TPU v7x, 512 devices: a whole 4x8x8 slice. The times are simulated.
512 devices in a mesh: chan: 8 (over z), space: 64 (over y, x, core).
Axes of the slice: x: 4, y: 8, z: 8, core: 2. Of those that a mesh axis runs over, the one named last changes fastest.
Arguments:
- cotangent: bfloat16 [80, 131072], P(None, 'space'), may hold values from -6 to 6
- pair_band: int32 [8192], P('space'), may hold values from 0 to 15
- pair_target: int32 [8192], P('space'), may hold values from 0 to 1023, as said below
- pair_count: int32 [64], P('space'), may hold values from 1 to 128, as said below
- pair_weight: bfloat16 [8192, 128, 128], P('space'), may hold values from -0.5 to 0.5
- head_weight: bfloat16 [512, 80], P('chan'), may hold values from -0.25 to 0.25
- features: bfloat16 [512, 131072], P('chan', 'space'), may hold values from -6 to 6
Outputs:
- feature_grad: bfloat16 [512, 131072], P('chan', 'space')
- weight_grad: float32 [512, 80], P('chan')
Inputs may be any that keep to these rules, and one draw needn't show every extreme that they name: `pair_target`: targets of the slots of one device fall on each device's blocks (device index = target // 16) exactly 2 times, so at most 2 live pairs go from one device to one device; the first and last device of space have all slots live. `pair_count`: devices near both ends of space carry more live pairs than those in the middle.
All inputs are finite; a program needn't handle non-finite values.
Results may differ from a plain program's by a relative error of at most 0.0058.
Values may be sent and summed in bfloat16 or wider, within the bound.
No kernel may reach another device: no remote copies, remote signals or barrier semaphores. Data moves between devices by JAX's collectives and lax.ppermute only.
A program may use at most 64 MiB of HBM per device.

v0:
```python
import jax
import jax.numpy as jnp
from jax import lax
from jax.sharding import PartitionSpec as P


def on_device(cotangent, pair_band, pair_target, pair_count, pair_weight, head_weight, features):
    nspace = lax.axis_size("space")
    vars_all = cotangent.shape[0]
    ll_local = cotangent.shape[1]
    block_size = pair_weight.shape[1]
    pair_slots = pair_band.shape[0]
    hp_local = features.shape[1]
    hp_blocks = hp_local // block_size
    per_peer = pair_slots // nspace
    band_blocks = cotangent.reshape(vars_all, ll_local // block_size, block_size).transpose(1, 0, 2)
    picked = band_blocks[pair_band]
    contrib = jnp.einsum(
        "pvr,prq->pvq", picked, pair_weight, preferred_element_type=jnp.float32
    ).astype(jnp.bfloat16)
    pair_index = jnp.arange(pair_slots)
    live_pair = pair_index < pair_count[0]
    dest_device = pair_target // hp_blocks
    local_block = pair_target % hp_blocks
    earlier = (
        (dest_device[:, None] == dest_device[None, :])
        & live_pair[None, :]
        & (pair_index[None, :] < pair_index[:, None])
    )
    slot_rank = jnp.sum(earlier.astype(jnp.int32), axis=1)
    slot_index = jnp.where(live_pair, dest_device * per_peer + slot_rank, pair_slots)
    sendbuf = (
        jnp.zeros((pair_slots, vars_all, block_size), jnp.bfloat16)
        .at[slot_index]
        .set(contrib, mode="drop")
    )
    labels = (
        jnp.full((pair_slots,), -1.0, jnp.bfloat16)
        .at[slot_index]
        .set(local_block.astype(jnp.bfloat16), mode="drop")
    )
    sendbuf = sendbuf.reshape(nspace, per_peer, vars_all, block_size)
    labels = labels.reshape(nspace, per_peer)
    received, received_tags = (
        lax.all_to_all(sendbuf, "space", split_axis=0, concat_axis=0, tiled=True),
        lax.all_to_all(labels, "space", split_axis=0, concat_axis=0, tiled=True),
    )
    block_ids = jnp.arange(hp_blocks).astype(jnp.bfloat16)
    onehot = (received_tags.reshape(pair_slots)[:, None] == block_ids[None, :]).astype(jnp.bfloat16)
    summed = jnp.einsum(
        "sh,svq->vhq",
        onehot,
        received.reshape(pair_slots, vars_all, block_size),
        preferred_element_type=jnp.float32,
    )
    pixel_part = summed.astype(jnp.bfloat16).reshape(vars_all, hp_local)
    feature_grad = jnp.dot(head_weight, pixel_part, preferred_element_type=jnp.float32).astype(
        jnp.bfloat16
    )
    partial_value = lax.dot_general(
        features, pixel_part, (((1,), (1,)), ((), ())), preferred_element_type=jnp.float32
    )
    grad_scale = float(hp_local * nspace) ** (-0.5)
    weight_grad = lax.psum(partial_value, "space") * grad_scale
    return (feature_grad, weight_grad)


def solution(mesh):
    placed = (
        P(None, "space"),
        P("space"),
        P("space"),
        P("space"),
        P("space", None, None),
        P("chan", None),
        P("chan", "space"),
    )
    return jax.shard_map(
        on_device,
        mesh=mesh,
        in_specs=placed,
        out_specs=(P("chan", "space"), P("chan", None)),
        check_vma=False,
    )
```

profile of v0, /device:TPU:1, one launch (start us, length us, event | category | flops | bytes accessed | tf_op | source)
XLA Modules:
  0.0 358.5 jit_solution(4748789527923973483)
XLA Ops:
  0.6 0.0 copy-start
  0.6 0.7 fusion.10
  2.0 0.2 convert_reduce_fusion
  2.2 1.3 scatter_custom_fusion.1
  3.6 0.8 all_to_all.12
  4.4 11.6 %all-to-all-start.1 = ((bf16[64,1,2]{2,1,0:T(2,128)(2,1)}), bf16[64,1,2]{2,1,0:T(2,128)(2,1)S(1)}, u32[]{:S(2)}, u32[]{:S(2)}) async-start(bf16[64,1,2]{2,1,0:T(2,128)(2,1)} %all_to_all.12), calls=%async_computation.1 | async-start | bytes 65536 | tf_op jit(solution)/shard_map/all_to_all | solution.py:46
  16.0 0.0 copy-done
  16.0 0.1 bitcast_bitcast_fusion
  16.0 0.7 compare_select_fusion
  16.7 1.1 gather_fusion
  17.8 5.2 %convolution_convert_fusion.1 = bf16[128,80,128]{2,1,0:T(8,128)(2,1)} fusion(bf16[128,80,128]{2,1,0:T(8,128)(2,1)S(1)} %gather_fusion, bf16[128,128,128]{2,1,0:T(8,128)(2,1)} %param.11), kind=kOutput, calls=%fused_computation.5 | convolution fusion | flops 336855040 | bytes 9437184 | tf_op jit(solution)/shard_map/pvr,prq->pvq/dot_general | solution.py:18
  23.0 0.3 broadcast_in_dim.12
  23.3 12.1 %scatter_fusion = bf16[128,80,128]{2,1,0:T(8,128)(2,1)S(1)} fusion(bf16[128,80,128]{2,1,0:T(8,128)(2,1)S(1)} %broadcast_in_dim.12, s32[128]{0:T(128)S(1)} %compare_select_fusion.1, bf16[128,80,128]{2,1,0:T(8,128)(2,1)} %convolution_convert_fusion.1), kind=kCustom, calls=%fused_computation.1 | custom fusion | bytes 7864832 | tf_op jit(solution)/shard_map/scatter | solution.py:35
  35.5 3.6 %copy.17 = bf16[64,2,80,128]{3,1,2,0:T(2,128)(2,1)} copy(bf16[64,2,80,128]{3,2,1,0:T(8,128)(2,1)S(1)} %bitcast.31) | data formatting | bytes 5242880 | tf_op jit(solution)/shard_map/reshape | solution.py:42
  39.1 0.0 all-to-all-done.1
  39.1 10.5 %all-to-all-start = ((bf16[64,2,80,128]{3,1,2,0:T(2,128)(2,1)}), bf16[64,2,80,128]{3,1,2,0:T(2,128)(2,1)S(1)}, u32[]{:S(2)}, u32[]{:S(2)}) async-start(bf16[64,2,80,128]{3,1,2,0:T(2,128)(2,1)} %copy.17), calls=%async_computation | async-start | bytes 5242880 | tf_op jit(solution)/shard_map/all_to_all | solution.py:45
  49.6 0.1 reduce
  49.7 0.1 eq.33
  49.8 60.6 %all-to-all-done = bf16[64,2,80,128]{3,1,2,0:T(2,128)(2,1)S(1)} async-done(((bf16[64,2,80,128]{3,1,2,0:T(2,128)(2,1)}), bf16[64,2,80,128]{3,1,2,0:T(2,128)(2,1)S(1)}, u32[]{:S(2)}, u32[]{:S(2)}) %all-to-all-start) | async-done | bytes 2621472 | tf_op jit(solution)/shard_map/all_to_all | solution.py:45
  110.4 2.9 copy.18
  113.3 0.0 copy-start.1
  113.3 0.0 copy-start.2
  113.4 0.5 convolution_convert_fusion.2
  113.9 0.2 copy-done.1
  114.1 0.9 fusion
  115.0 0.0 copy-done.2
  115.0 0.2 convolution_bitcast_fusion
  115.2 242.7 %psum.7 = f32[64,80]{1,0:T(8,128)S(1)} all-reduce(f32[64,80]{1,0:T(8,128)S(1)} %convolution_bitcast_fusion), channel_id=1, replica_groups=mesh['chan'=8,'space'=64] {'space'}, use_global_device_ids=true, to_apply=%region_3.4 | all-reduce | flops 5120 | bytes 40960 | tf_op jit(solution)/shard_map/psum | solution.py:64
  357.9 0.6 broadcast_multiply_fusion
  (4 shorter events, 0.0 us)
Async XLA Ops:
  0.6 15.3 %copy-start = (bf16[80,2048]{1,0:T(8,128)(2,1)S(1)}, bf16[80,2048]{1,0:T(8,128)(2,1)}, u32[]{:S(2)}) copy-start(bf16[80,2048]{1,0:T(8,128)(2,1)} %param.7) | copy-start | bytes 983044
  4.4 34.7 %all-to-all-start.1 = ((bf16[64,1,2]{2,1,0:T(2,128)(2,1)}), bf16[64,1,2]{2,1,0:T(2,128)(2,1)S(1)}, u32[]{:S(2)}, u32[]{:S(2)}) async-start(bf16[64,1,2]{2,1,0:T(2,128)(2,1)} %all_to_all.12), calls=%async_computation.1 | async-start | bytes 65536 | tf_op jit(solution)/shard_map/all_to_all | solution.py:46
  39.1 71.3 %all-to-all-start = ((bf16[64,2,80,128]{3,1,2,0:T(2,128)(2,1)}), bf16[64,2,80,128]{3,1,2,0:T(2,128)(2,1)S(1)}, u32[]{:S(2)}, u32[]{:S(2)}) async-start(bf16[64,2,80,128]{3,1,2,0:T(2,128)(2,1)} %copy.17), calls=%async_computation | async-start | bytes 5242880 | tf_op jit(solution)/shard_map/all_to_all | solution.py:45
  113.3 0.7 copy-start.1
  113.3 1.6 copy-start.2
where the time goes:
time: 363 us; the launch traced here: 359 us
  blocking collectives  243 us (67%)
  waiting for transfers between devices  60.6 us (17%)
  local copies, waits for them, and re-layouts  22.6 us (6%)
  starting transfers between devices  22.1 us (6%)
  matrix products  6.88 us (2%)
    psum x1, blocking collectives, on_device(): weight_grad = lax.psum(partial_value, 'space') * grad_scale  243 us
    all_to_all x1, waiting for transfers between devices, on_device(): lax.all_to_all(sendbuf, 'space', split_axis=0, concat_axis=0, tiled=True)  60.6 us
    scatter x1, local copies, waits for them, and re-layouts, on_device(): sendbuf = jnp.zeros((pair_slots, vars_all, block_size), jnp.bfloat16).at[...  12.1 us
    all_to_all x1, starting transfers between devices, on_device(): lax.all_to_all(labels, 'space', split_axis=0, concat_axis=0, tiled=True)  11.6 us
    all_to_all x1, starting transfers between devices, on_device(): lax.all_to_all(sendbuf, 'space', split_axis=0, concat_axis=0, tiled=True)  10.5 us
  transfers between devices with their start and end apart: 2, of which 1 were waited for; matrix products, arithmetic and copies ran while one was open for 7% of the time, Pallas kernels for 0%

commit v1 on v0

v1 whole, which is shorter than its diff:
```python
import functools

import jax
import jax.numpy as jnp
import numpy as np
from jax import lax
from jax.experimental import pallas as pl
from jax.experimental.pallas import tpu as pltpu
from jax.sharding import Mesh
from jax.sharding import PartitionSpec as P

NCHAN = 8
NSPACE = 64
VARS = 80
B = 128
SLOTS = 128
BLOCKS = 16
OWN = VARS // NCHAN
MSG = 24
CHUNK = 16
PART = OWN * BLOCKS
GROUP = 8
SPACE = ("y", "x", "core")
F32 = jnp.float32
BF16 = jnp.bfloat16


def contribute(band, target, count, place, cot, weight, out, lhs, acc, seen):
    step = pl.program_id(0)
    mine = place[0] // NSPACE
    space = place[0] % NSPACE

    @pl.when(step == 0)
    def _():
        for j in range(NSPACE):
            seen[j] = 0
        row = lax.broadcasted_iota(jnp.int32, (32, VARS), 0)
        col = lax.broadcasted_iota(jnp.int32, (32, VARS), 1)
        low = row & 15
        tail = low - 8 - 2 * (row >> 4)
        var = jnp.where(low < 8, low, jnp.where((tail >= 0) & (tail < 2), 8 + tail, -VARS * NCHAN))
        pick = jnp.where(col == var + mine * OWN, 1.0, 0.0).astype(BF16)
        rows = jnp.dot(pick, cot[...], preferred_element_type=F32).astype(BF16)
        for j in range(BLOCKS):
            for rank in range(2):
                lhs[2 * j + rank] = rows[16 * rank : 16 * rank + 16, j * B : (j + 1) * B]

    tag_row = lax.broadcasted_iota(jnp.int32, (8, B), 0)
    tag_lane = lax.broadcasted_iota(jnp.int32, (8, B), 1)
    tag_lane = jnp.where(tag_row == 4, tag_lane, -1)
    for i in range(CHUNK):
        slot = step * CHUNK + i
        dest = target[slot] >> 4
        rank = seen[dest]
        seen[dest] = rank + 1
        live = slot < count[0]
        value = jnp.dot(lhs[2 * band[slot] + rank], weight[i], preferred_element_type=F32)
        value = jnp.where(live, value, 0.0)
        tag = jnp.where(live, (target[slot] & 15) + 1, 0).astype(F32)
        extra = value[8:16] + jnp.where(tag_lane == 2 * space + rank, tag, 0.0)
        acc[dest, pl.ds(pl.multiple_of(8 * rank, 8), 8), :] = value[0:8]
        acc[dest, pl.ds(pl.multiple_of(16 + 8 * rank, 8), 8), :] = extra

    @pl.when(step == pl.num_programs(0) - 1)
    def _():
        def emit(k, carry):
            parts = []
            for half in range(2):
                x = acc[2 * k + half]
                parts += [x[0:16], x[16:24] + x[24:32]]
            rows = jnp.concatenate(parts, axis=0).astype(BF16)
            out[pl.ds(pl.multiple_of(2 * MSG * k, 2 * MSG), 2 * MSG), :] = rows
            return carry

        lax.fori_loop(0, NSPACE // 2, emit, 0, unroll=4)


def collect(got, tag_pick, spread, coef, out):
    x = got[...]
    tags = jnp.dot(tag_pick[...], x, preferred_element_type=F32).astype(BF16)
    label = jnp.dot(tags, spread[...], preferred_element_type=F32)[0:1]
    goal = jnp.where(label > 0.5, label * coef[0:1] + coef[1:2], -1.0)
    row = lax.broadcasted_iota(jnp.int32, (PART, NSPACE * MSG), 0).astype(F32)
    route = jnp.where(row == goal, 1.0, 0.0).astype(BF16)
    part = jnp.dot(route, x, preferred_element_type=F32).astype(BF16)
    for j in range(NCHAN):
        out[j] = part


def heads(parts, features, head, proj, fold, grad, share, wide):
    row = lax.broadcasted_iota(jnp.int32, (16, B), 0)
    main = [jnp.where((row >> 3) == k, 1.0, 0.0).astype(BF16) for k in range(2)]
    tail = [jnp.where((row >> 1) == k, 1.0, 0.0).astype(BF16) for k in range(8)]
    for b in range(BLOCKS):
        for c in range(NCHAN):
            base = PART * c + 32 + 16 * (b // 2)
            wide[16 * c : 16 * c + 16, b * B : (b + 1) * B] = parts[base : base + 16] * main[b % 2]
            base = PART * c + 16 * (b // 8)
            wide[128 + 16 * c : 144 + 16 * c, b * B : (b + 1) * B] = (
                parts[base : base + 16] * tail[b % 8]
            )
    k = wide[...]
    total = lax.dot_general(
        features[...], k, (((1,), (1,)), ((), ())), preferred_element_type=F32
    )
    total = jnp.dot(total, fold[...], preferred_element_type=F32, precision=lax.Precision.HIGHEST)
    for j in range(GROUP):
        share[j] = total
    lifted = jnp.dot(head[...], proj[...], preferred_element_type=F32).astype(BF16)
    grad[...] = jnp.dot(lifted, k, preferred_element_type=F32).astype(BF16)


def add_copies(got, out):
    total = got[0]
    for j in range(1, GROUP):
        total = total + got[j]
    for j in range(GROUP):
        out[j] = total


def add_last(scale, got, out):
    total = got[0]
    for j in range(1, GROUP):
        total = total + got[j]
    out[...] = (total * scale)[:, 0:VARS]


def tables():
    j = np.arange(NSPACE * MSG)
    src, t, r = j // MSG, (j % MSG) // 8, j % 8
    rank = np.where(t < 2, t, r // 2)
    data = (t < 2) | (r < 4)
    tag_pick = np.zeros((16, j.size), np.float32)
    tag_pick[0] = (t == 2) & (r == 4)
    spread = (np.arange(SLOTS)[:, None] == (2 * src + rank)[None]) & data[None]
    coef = np.zeros((8, j.size), np.float32)
    coef[0] = np.where(t < 2, 8, 2)
    coef[1] = np.where(t < 2, 32 - 8 + r, -2 + (r & 1))
    k = np.arange(256)
    c, i = (k % 128) // 16, k % 16
    var = OWN * c + np.where(k < 128, i % 8, 8 + i % 2)
    proj = np.arange(VARS)[:, None] == var[None]
    fold = var[:, None] == np.arange(B)[None]
    return (
        tag_pick.astype(BF16),
        spread.astype(BF16),
        coef,
        proj.astype(BF16),
        fold.astype(np.float32),
    )


def whole(shape):
    return jax.ShapeDtypeStruct(*shape)


def on_device(cotangent, pair_band, pair_target, pair_count, pair_weight, head_weight, features):
    tag_pick, spread, coef, proj, fold = tables()
    hp_local = features.shape[1]
    place = lax.axis_index(("chan",) + SPACE).astype(jnp.int32).reshape(1)
    sent = pl.pallas_call(
        contribute,
        out_shape=jax.ShapeDtypeStruct((NSPACE * MSG, B), BF16),
        grid_spec=pltpu.PrefetchScalarGridSpec(
            num_scalar_prefetch=4,
            grid=(SLOTS // CHUNK,),
            in_specs=[
                pl.BlockSpec((VARS, BLOCKS * B), lambda i, *_: (0, 0)),
                pl.BlockSpec((CHUNK, B, B), lambda i, *_: (i, 0, 0)),
            ],
            out_specs=pl.BlockSpec((NSPACE * MSG, B), lambda i, *_: (0, 0)),
            scratch_shapes=[
                pltpu.VMEM((2 * BLOCKS, 16, B), BF16),
                pltpu.VMEM((NSPACE, 32, B), F32),
                pltpu.SMEM((NSPACE,), jnp.int32),
            ],
        ),
        name="contribute",
    )(pair_band, pair_target, pair_count, place, cotangent, pair_weight)
    got = lax.all_to_all(sent.reshape(NSPACE, MSG, B), SPACE, 0, 0, tiled=True)
    parts = pl.pallas_call(
        collect,
        out_shape=jax.ShapeDtypeStruct((NCHAN, PART, B), BF16),
        name="collect",
    )(got.reshape(NSPACE * MSG, B), tag_pick, spread, coef)
    parts = lax.all_to_all(parts, "chan", 0, 0, tiled=True)
    feature_grad, share = pl.pallas_call(
        heads,
        out_shape=(
            jax.ShapeDtypeStruct((head_weight.shape[0], hp_local), BF16),
            jax.ShapeDtypeStruct((GROUP, head_weight.shape[0], B), F32),
        ),
        scratch_shapes=[pltpu.VMEM((256, hp_local), BF16)],
        name="heads",
    )(parts.reshape(NCHAN * PART, B), features, head_weight, proj, fold)
    share = lax.all_to_all(share, ("x", "core"), 0, 0, tiled=True)
    share = pl.pallas_call(
        add_copies, out_shape=jax.ShapeDtypeStruct(share.shape, F32), name="add_copies"
    )(share)
    share = lax.all_to_all(share, "y", 0, 0, tiled=True)
    grad_scale = float(hp_local * NSPACE) ** (-0.5)
    weight_grad = pl.pallas_call(
        functools.partial(add_last, grad_scale),
        out_shape=jax.ShapeDtypeStruct(head_weight.shape, F32),
        name="add_last",
    )(share)
    return feature_grad, weight_grad


def solution(mesh):
    fine = Mesh(mesh.devices.reshape(NCHAN, 8, 4, 2), ("chan",) + SPACE)
    placed = (
        P(None, SPACE),
        P(SPACE),
        P(SPACE),
        P(SPACE),
        P(SPACE, None, None),
        P("chan", None),
        P("chan", SPACE),
    )
    return jax.shard_map(
        on_device,
        mesh=fine,
        in_specs=placed,
        out_specs=(P("chan", SPACE), P("chan", None)),
        check_vma=False,
    )
```

time: 363 us -> 94.3 us (0.26); the launches traced: 359 us -> 93.5 us
  blocking collectives: 243 us -> 76.1 us
  waiting for transfers between devices: 60.6 us -> 0 us
  local copies, waits for them, and re-layouts: 22.6 us -> 0 us
  starting transfers between devices: 22.1 us -> 0 us
  Pallas kernels: 0 us -> 16.1 us
  matrix products: 6.88 us -> 0 us
    psum x1 -> x0, blocking collectives: 243 us -> none  [on_device(): weight_grad = lax.psum(partial_value, 'space') * grad_scale]
    all_to_all x0 -> x4, blocking collectives: none -> 76.1 us  [the longest x1 26.9 us: on_device(): got = lax.all_to_all(sent.reshape(NSPACE, MSG, B), SPACE, 0, 0, tiled=True)]
    all_to_all x2 -> x0, waiting for transfers between devices: 60.6 us -> none  [the longest x1 60.6 us: on_device(): lax.all_to_all(sendbuf, 'space', split_axis=0, concat_axis=0, tiled=True)]
    all_to_all x2 -> x0, starting transfers between devices: 22.1 us -> none  [the longest x1 11.6 us: on_device(): lax.all_to_all(labels, 'space', split_axis=0, concat_axis=0, tiled=True)]
    pallas_call x0 -> x5, Pallas kernels: none -> 16.1 us  [the longest x1 7.35 us: on_device(): pl.pallas_call(contribute, out_shape=jax.ShapeDtypeStruct((NSPACE * MSG,...]
    scatter x2 -> x0, local copies, waits for them, and re-layouts: 13.5 us -> none  [the longest x1 12.1 us: on_device(): sendbuf = jnp.zeros((pair_slots, vars_all, block_size), jnp.bfloat16).at[...]
    dot_general x4 -> x0, matrix products: 6.88 us -> none  [the longest x1 5.22 us: on_device(): jnp.einsum('pvr,prq->pvq', picked, pair_weight, preferred_element_type=jn...]
    all_to_all x2 -> x0, local copies, waits for them, and re-layouts: 3.69 us -> none  [the longest x1 2.9 us: on_device(): lax.all_to_all(sendbuf, 'space', split_axis=0, concat_axis=0, tiled=True)]
  transfers between devices with their start and end apart: 2 -> 0, of which waited for: 1 -> 0; matrix products, arithmetic and copies ran while one was open for 7% -> 0% of each run, Pallas kernels for 0% -> 0%
where the time goes in v1:
time: 94.3 us; the launch traced here: 93.5 us
  blocking collectives  76.1 us (81%)
  Pallas kernels  16.1 us (17%)
  between operations  1.29 us (1%)
    all_to_all x1, blocking collectives, on_device(): got = lax.all_to_all(sent.reshape(NSPACE, MSG, B), SPACE, 0, 0, tiled=True)  26.9 us
    all_to_all x1, blocking collectives, on_device(): parts = lax.all_to_all(parts, 'chan', 0, 0, tiled=True)  22.8 us
    all_to_all x1, blocking collectives, on_device(): share = lax.all_to_all(share, 'y', 0, 0, tiled=True)  14.3 us
    all_to_all x1, blocking collectives, on_device(): share = lax.all_to_all(share, ('x', 'core'), 0, 0, tiled=True)  12 us
    pallas_call x1, Pallas kernels, on_device(): pl.pallas_call(contribute, out_shape=jax.ShapeDtypeStruct((NSPACE * MSG,...  7.35 us
    pallas_call x1, Pallas kernels, on_device(): pl.pallas_call(heads, out_shape=(jax.ShapeDtypeStruct((head_weight.shape[...  3.1 us
    pallas_call x1, Pallas kernels, on_device(): pl.pallas_call(collect, out_shape=jax.ShapeDtypeStruct((NCHAN, PART, B),...  2.44 us

profile of v1, /device:TPU:1, one launch (start us, length us, event | category | flops | bytes accessed | tf_op | source)
XLA Modules:
  0.0 93.5 jit_solution(10122275726552210935)
XLA Ops:
  1.3 7.4 %contribute.1 = bf16[1536,128]{1,0:T(8,128)(2,1)} custom-call(s32[128]{0:T(128)} %band.1, s32[128]{0:T(128)} %target.1, s32[1]{0:T(128)S(6)} %copy.14.count, s32[1]{0:T(128)} %bitcast.place, bf16[80,2048]{1,0:T(8,128)(2,1)} %cot.1, bf16[128,128,128]{2,1,0:T(8,128)(2,1)} %weight.1), custom_call_target="tpu_custom_call" | custom-call | tf_op jit(solution)/shard_map/contribute/pallas_call | solution.py:161
  8.6 26.9 %all_to_all.20 = bf16[64,24,128]{2,1,0:T(8,128)(2,1)} all-to-all(bf16[64,24,128]{2,1,0:T(8,128)(2,1)} %bitcast.4), channel_id=1, replica_groups=mesh['chan'=8,'y'=8,'x'=4,'core'=2] {'y','x','core'}, dimensions={0} | all-to-all | bytes 786432 | tf_op jit(solution)/shard_map/all_to_all | solution.py:180
  35.6 2.4 %collect.1 = bf16[8,160,128]{2,1,0:T(8,128)(2,1)} custom-call(bf16[1536,128]{1,0:T(8,128)(2,1)} %bitcast.5, bf16[16,1536]{1,0:T(8,128)(2,1)} %constant.32.clone.tag_pick, bf16[128,1536]{1,0:T(8,128)(2,1)} %constant.33.clone.spread, f32[8,1536]{1,0:T(8,128)} %constant.34.clone.coef), custom_call_target="tpu_custom_call" | custom-call | tf_op jit(solution)/shard_map/collect/pallas_call | solution.py:181
  38.0 22.8 %all_to_all.21 = bf16[8,160,128]{2,1,0:T(8,128)(2,1)} all-to-all(bf16[8,160,128]{2,1,0:T(8,128)(2,1)} %collect.1), channel_id=1, replica_groups=mesh['chan'=8,'y'=8,'x'=4,'core'=2] {'chan'}, dimensions={0} | all-to-all | bytes 655360 | tf_op jit(solution)/shard_map/all_to_all | solution.py:186
  60.9 3.1 %heads.1 = (bf16[64,2048]{1,0:T(8,128)(2,1)}, f32[8,64,128]{2,1,0:T(8,128)}) custom-call(bf16[1280,128]{1,0:T(8,128)(2,1)} %bitcast.6, bf16[64,2048]{1,0:T(8,128)(2,1)} %features.1, bf16[64,80]{1,0:T(8,128)(2,1)} %head.1, bf16[80,256]{1,0:T(8,128)(2,1)} %constant.35.clone.proj, f32[256,128]{1,0:T(8,128)} %constant.36.clone.fold), custom_call_target="tpu_custom_call" | custom-call | tf_op jit(solution)/shard_map/heads/pallas_call | solution.py:187
  64.0 12.0 %all_to_all.22.got = f32[8,64,128]{2,1,0:T(8,128)} all-to-all(f32[8,64,128]{2,1,0:T(8,128)} %get-tuple-element.5), channel_id=1, replica_groups=mesh['chan'=8,'y'=8,'x'=4,'core'=2] {'x','core'}, dimensions={0} | all-to-all | bytes 524288 | tf_op jit(solution)/shard_map/all_to_all | solution.py:196
  75.9 1.7 %add_copies.1 = f32[8,64,128]{2,1,0:T(8,128)} custom-call(f32[8,64,128]{2,1,0:T(8,128)} %all_to_all.22.got), custom_call_target="tpu_custom_call" | custom-call | tf_op jit(solution)/shard_map/add_copies/pallas_call | solution.py:197
  77.6 14.3 %all_to_all.23.got = f32[8,64,128]{2,1,0:T(8,128)} all-to-all(f32[8,64,128]{2,1,0:T(8,128)} %add_copies.1), channel_id=1, replica_groups=mesh['chan'=8,'y'=8,'x'=4,'core'=2] {'y'}, dimensions={0} | all-to-all | bytes 524288 | tf_op jit(solution)/shard_map/all_to_all | solution.py:200
  91.9 1.6 %add_last.1 = f32[64,80]{1,0:T(8,128)} custom-call(f32[8,64,128]{2,1,0:T(8,128)} %all_to_all.23.got), custom_call_target="tpu_custom_call" | custom-call | tf_op jit(solution)/shard_map/add_last/pallas_call | solution.py:202

commit v2 on v1

v2 whole, which is shorter than its diff:
```python
import functools

import jax
import jax.numpy as jnp
import numpy as np
from jax import lax
from jax.experimental import pallas as pl
from jax.experimental.pallas import tpu as pltpu
from jax.sharding import Mesh
from jax.sharding import PartitionSpec as P

NCHAN = 8
NSPACE = 64
VARS = 80
B = 128
SLOTS = 128
BLOCKS = 16
OWN = VARS // NCHAN
MSG = 24
CHUNK = 16
PART = OWN * BLOCKS
GROUP = 8
SPACE = ("y", "x", "core")
F32 = jnp.float32
BF16 = jnp.bfloat16


def contribute(
    place, count, band_in, target_in, cot_in, weight_in, out, band, target, cot, weight, lhs, acc, seen, sems,
):
    chunks = SLOTS // CHUNK
    small = [
        pltpu.make_async_copy(src, dst, sems.at[chunks + k])
        for k, (src, dst) in enumerate(
            ((cot_in, cot), (band_in, band), (target_in, target))
        )
    ]
    parts = [
        pltpu.make_async_copy(
            weight_in.at[pl.ds(k * CHUNK, CHUNK)], weight.at[pl.ds(k * CHUNK, CHUNK)], sems.at[k]
        )
        for k in range(chunks)
    ]
    for copy in small:
        copy.start()
    for copy in parts:
        copy.start()
    mine = place[0] // NSPACE
    space = place[0] % NSPACE
    for j in range(NSPACE):
        seen[j] = 0
    row = lax.broadcasted_iota(jnp.int32, (32, VARS), 0)
    col = lax.broadcasted_iota(jnp.int32, (32, VARS), 1)
    low = row & 15
    tail = low - 8 - 2 * (row >> 4)
    var = jnp.where(low < 8, low, jnp.where((tail >= 0) & (tail < 2), 8 + tail, -VARS * NCHAN))
    pick = jnp.where(col == var + mine * OWN, 1.0, 0.0).astype(BF16)
    tag_row = lax.broadcasted_iota(jnp.int32, (8, B), 0)
    tag_lane = lax.broadcasted_iota(jnp.int32, (8, B), 1)
    tag_lane = jnp.where(tag_row == 4, tag_lane, -1)
    small[0].wait()
    rows = jnp.dot(pick, cot[...], preferred_element_type=F32).astype(BF16)
    for j in range(BLOCKS):
        for rank in range(2):
            lhs[2 * j + rank] = rows[16 * rank : 16 * rank + 16, j * B : (j + 1) * B]
    for copy in small[1:]:
        copy.wait()

    def chunk(k, carry):
        base = k * CHUNK
        pltpu.make_async_copy(
            weight_in.at[pl.ds(base, CHUNK)], weight.at[pl.ds(base, CHUNK)], sems.at[k]
        ).wait()
        for i in range(CHUNK):
            slot = base + i
            dest = target[slot] >> 4
            rank = seen[dest]
            seen[dest] = rank + 1
            live = slot < count[0]
            value = jnp.dot(lhs[2 * band[slot] + rank], weight[slot], preferred_element_type=F32)
            value = jnp.where(live, value, 0.0)
            tag = jnp.where(live, (target[slot] & 15) + 1, 0).astype(F32)
            extra = value[8:16] + jnp.where(tag_lane == 2 * space + rank, tag, 0.0)
            acc[dest, pl.ds(pl.multiple_of(8 * rank, 8), 8), :] = value[0:8]
            acc[dest, pl.ds(pl.multiple_of(16 + 8 * rank, 8), 8), :] = extra
        return carry

    lax.fori_loop(0, chunks, chunk, 0)

    def emit(k, carry):
        parts = []
        for half in range(2):
            x = acc[2 * k + half]
            parts += [x[0:16], x[16:24] + x[24:32]]
        rows = jnp.concatenate(parts, axis=0).astype(BF16)
        out[pl.ds(pl.multiple_of(2 * MSG * k, 2 * MSG), 2 * MSG), :] = rows
        return carry

    lax.fori_loop(0, NSPACE // 2, emit, 0, unroll=4)


def collect(got, tag_pick, spread, coef, out):
    x = got[...]
    tags = jnp.dot(tag_pick[...], x, preferred_element_type=F32).astype(BF16)
    label = jnp.dot(tags, spread[...], preferred_element_type=F32)[0:1]
    goal = jnp.where(label > 0.5, label * coef[0:1] + coef[1:2], -1.0)
    row = lax.broadcasted_iota(jnp.int32, (PART, NSPACE * MSG), 0).astype(F32)
    route = jnp.where(row == goal, 1.0, 0.0).astype(BF16)
    part = jnp.dot(route, x, preferred_element_type=F32).astype(BF16)
    for j in range(NCHAN):
        out[j] = part


def widen(parts, wide):
    row = lax.broadcasted_iota(jnp.int32, (16, B), 0)
    main = [jnp.where((row >> 3) == k, 1.0, 0.0).astype(BF16) for k in range(2)]
    tail = [jnp.where((row >> 1) == k, 1.0, 0.0).astype(BF16) for k in range(8)]
    for b in range(BLOCKS):
        for c in range(NCHAN):
            base = PART * c + 32 + 16 * (b // 2)
            wide[16 * c : 16 * c + 16, b * B : (b + 1) * B] = parts[base : base + 16] * main[b % 2]
            base = PART * c + 16 * (b // 8)
            wide[128 + 16 * c : 144 + 16 * c, b * B : (b + 1) * B] = (
                parts[base : base + 16] * tail[b % 8]
            )


def weight_share(parts, features, fold, share, wide):
    widen(parts, wide)
    total = lax.dot_general(
        features[...], wide[...], (((1,), (1,)), ((), ())), preferred_element_type=F32
    )
    total = jnp.dot(total, fold[...], preferred_element_type=F32, precision=lax.Precision.HIGHEST)
    lane = lax.broadcasted_iota(jnp.int32, (64, B), 1)
    low = jnp.where(lane < 64, total, 0.0)
    high = jnp.where(lane < 64, 0.0, total)
    front = low[0:32] + pltpu.roll(low[32:64], 64, 1)
    back = high[32:40]
    for k in range(8):
        if k != 4:
            back = back + pltpu.roll(high[8 * k : 8 * k + 8], (16 * k - 64) % B, 1)
    for j in range(GROUP):
        share[j, 0:32] = front
        share[j, 32:40] = back


def feature_part(parts, head, proj, grad, wide):
    widen(parts, wide)
    lifted = jnp.dot(head[...], proj[...], preferred_element_type=F32).astype(BF16)
    grad[...] = jnp.dot(lifted, wide[...], preferred_element_type=F32).astype(BF16)


def add_up(got):
    total = got[0]
    for j in range(1, GROUP):
        total = total + got[j]
    return total


def add_copies(got, out):
    total = add_up(got)
    for j in range(GROUP):
        out[j] = total


def add_last(scale, got, out):
    total = add_up(got) * scale
    front, back = total[0:32], total[32:40]
    out[0:32, 0:64] = front[:, 0:64]
    out[32:64, 0:64] = pltpu.roll(front, 64, 1)[:, 0:64]
    for k in range(8):
        out[8 * k : 8 * k + 8, 64:VARS] = pltpu.roll(back, (64 - 16 * k) % B, 1)[:, 64:VARS]


def tables():
    j = np.arange(NSPACE * MSG)
    src, t, r = j // MSG, (j % MSG) // 8, j % 8
    rank = np.where(t < 2, t, r // 2)
    data = (t < 2) | (r < 4)
    tag_pick = np.zeros((16, j.size), np.float32)
    tag_pick[0] = (t == 2) & (r == 4)
    spread = (np.arange(SLOTS)[:, None] == (2 * src + rank)[None]) & data[None]
    coef = np.zeros((8, j.size), np.float32)
    coef[0] = np.where(t < 2, 8, 2)
    coef[1] = np.where(t < 2, 32 - 8 + r, -2 + (r & 1))
    k = np.arange(256)
    c, i = (k % 128) // 16, k % 16
    var = OWN * c + np.where(k < 128, i % 8, 8 + i % 2)
    proj = np.arange(VARS)[:, None] == var[None]
    fold = var[:, None] == np.arange(B)[None]
    return (
        tag_pick.astype(BF16),
        spread.astype(BF16),
        coef,
        proj.astype(BF16),
        fold.astype(np.float32),
    )


def small_grant(mib):
    return pltpu.CompilerParams(vmem_limit_bytes=mib << 20)


def near(x):
    return pltpu.with_memory_space_constraint(x, pltpu.VMEM)


def far(x):
    return pltpu.with_memory_space_constraint(x, pltpu.HBM)


def on_device(cotangent, pair_band, pair_target, pair_count, pair_weight, head_weight, features):
    tag_pick, spread, coef, proj, fold = tables()
    hp_local = features.shape[1]
    place = lax.axis_index(("chan",) + SPACE).astype(jnp.int32).reshape(1)
    hbm = pl.BlockSpec(memory_space=pltpu.HBM)
    sent = pl.pallas_call(
        contribute,
        out_shape=jax.ShapeDtypeStruct((NSPACE * MSG, B), BF16),
        in_specs=[pl.BlockSpec(memory_space=pltpu.SMEM)] * 2 + [hbm] * 4,
        scratch_shapes=[
            pltpu.SMEM((SLOTS,), jnp.int32),
            pltpu.SMEM((SLOTS,), jnp.int32),
            pltpu.VMEM((VARS, BLOCKS * B), BF16),
            pltpu.VMEM((SLOTS, B, B), BF16),
            pltpu.VMEM((2 * BLOCKS, 16, B), BF16),
            pltpu.VMEM((NSPACE, 32, B), F32),
            pltpu.SMEM((NSPACE,), jnp.int32),
            pltpu.SemaphoreType.DMA((SLOTS // CHUNK + 3,)),
        ],
        compiler_params=small_grant(12),
        name="contribute",
    )(place, pair_count, *map(far, (pair_band, pair_target, cotangent, pair_weight)))
    got = lax.all_to_all(sent.reshape(NSPACE, MSG, B), SPACE, 0, 0, tiled=True)
    parts = pl.pallas_call(
        collect,
        out_shape=jax.ShapeDtypeStruct((NCHAN, PART, B), BF16),
        compiler_params=small_grant(8),
        name="collect",
    )(near(got.reshape(NSPACE * MSG, B)), tag_pick, spread, coef)
    parts = lax.all_to_all(parts, "chan", 0, 0, tiled=True).reshape(NCHAN * PART, B)
    parts = near(parts)
    share = pl.pallas_call(
        weight_share,
        out_shape=jax.ShapeDtypeStruct((GROUP, 40, B), F32),
        scratch_shapes=[pltpu.VMEM((256, hp_local), BF16)],
        compiler_params=small_grant(8),
        name="weight_share",
    )(parts, features, fold)
    share = lax.all_to_all(share, ("x", "core"), 0, 0, tiled=True)
    feature_grad = pl.pallas_call(
        feature_part,
        out_shape=jax.ShapeDtypeStruct((head_weight.shape[0], hp_local), BF16),
        scratch_shapes=[pltpu.VMEM((256, hp_local), BF16)],
        compiler_params=small_grant(8),
        name="feature_part",
    )(parts, head_weight, proj)
    share = pl.pallas_call(
        add_copies,
        out_shape=jax.ShapeDtypeStruct(share.shape, F32),
        compiler_params=small_grant(2),
        name="add_copies",
    )(near(share))
    share = lax.all_to_all(share, "y", 0, 0, tiled=True)
    grad_scale = float(hp_local * NSPACE) ** (-0.5)
    weight_grad = pl.pallas_call(
        functools.partial(add_last, grad_scale),
        out_shape=jax.ShapeDtypeStruct(head_weight.shape, F32),
        compiler_params=small_grant(2),
        name="add_last",
    )(near(share))
    return feature_grad, weight_grad


def solution(mesh):
    fine = Mesh(mesh.devices.reshape(NCHAN, 8, 4, 2), ("chan",) + SPACE)
    placed = (
        P(None, SPACE),
        P(SPACE),
        P(SPACE),
        P(SPACE),
        P(SPACE, None, None),
        P("chan", None),
        P("chan", SPACE),
    )
    return jax.shard_map(
        on_device,
        mesh=fine,
        in_specs=placed,
        out_specs=(P("chan", SPACE), P("chan", None)),
        check_vma=False,
    )
```

time: 94.3 us -> 78.9 us (0.84)
  blocking collectives: 76.1 us -> 59.4 us
  Pallas kernels: 16.1 us -> 7.27 us
  waiting for transfers between devices: 0 us -> 7.05 us
  starting transfers between devices: 0 us -> 3.38 us
    all_to_all x2 -> x1, blocking collectives: 37.2 us -> 22.6 us  [on_device(): lax.all_to_all(parts, 'chan', 0, 0, tiled=True).reshape(NCHAN * PART, B)]
    all_to_all x0 -> x1, waiting for transfers between devices: none -> 7.05 us  [on_device(): share = lax.all_to_all(share, 'y', 0, 0, tiled=True)]
    pallas_call x1, Pallas kernels: 7.35 us -> 3.41 us  [on_device(): pl.pallas_call(contribute, out_shape=jax.ShapeDtypeStruct((NSPACE * MSG,...]
    all_to_all x0 -> x1, starting transfers between devices: none -> 3.38 us  [on_device(): share = lax.all_to_all(share, 'y', 0, 0, tiled=True)]
    pallas_call x1, Pallas kernels: 2.44 us -> 0.56 us  [on_device(): pl.pallas_call(collect, out_shape=jax.ShapeDtypeStruct((NCHAN, PART, B),...]
    all_to_all x1, blocking collectives: 12 us -> 10.2 us  [on_device(): share = lax.all_to_all(share, ('x', 'core'), 0, 0, tiled=True)]
    pallas_call x1 -> x2, Pallas kernels: 3.1 us -> 1.93 us  [the longest x1 1.12 us: on_device(): pl.pallas_call(feature_part, out_shape=jax.ShapeDtypeStruct((head_weight....]
    pallas_call x1, Pallas kernels: 1.67 us -> 0.67 us  [on_device(): pl.pallas_call(add_copies, out_shape=jax.ShapeDtypeStruct(share.shape, F3...]
  transfers between devices with their start and end apart: 0 -> 1, of which waited for: 0 -> 1; matrix products, arithmetic and copies ran while one was open for 0% -> 0% of each run, Pallas kernels for 0% -> 1%
where the time goes in v2:
time: 78.9 us; the launch traced here: 78.6 us
  blocking collectives  59.4 us (75%)
  Pallas kernels  7.27 us (9%)
  waiting for transfers between devices  7.05 us (9%)
  starting transfers between devices  3.38 us (4%)
  between operations  1.47 us (2%)
    all_to_all x1, blocking collectives, on_device(): got = lax.all_to_all(sent.reshape(NSPACE, MSG, B), SPACE, 0, 0, tiled=True)  26.6 us
    all_to_all x1, blocking collectives, on_device(): lax.all_to_all(parts, 'chan', 0, 0, tiled=True).reshape(NCHAN * PART, B)  22.6 us
    all_to_all x1, blocking collectives, on_device(): share = lax.all_to_all(share, ('x', 'core'), 0, 0, tiled=True)  10.2 us
    all_to_all x1, waiting for transfers between devices, on_device(): share = lax.all_to_all(share, 'y', 0, 0, tiled=True)  7.05 us
    pallas_call x1, Pallas kernels, on_device(): pl.pallas_call(contribute, out_shape=jax.ShapeDtypeStruct((NSPACE * MSG,...  3.41 us
    all_to_all x1, starting transfers between devices, on_device(): share = lax.all_to_all(share, 'y', 0, 0, tiled=True)  3.38 us
  transfers between devices with their start and end apart: 1, of which 1 were waited for; matrix products, arithmetic and copies ran while one was open for 0% of the time, Pallas kernels for 1%

profile of v2, /device:TPU:1, one launch (start us, length us, event | category | flops | bytes accessed | tf_op | source)
XLA Modules:
  0.0 78.6 jit_solution(398093136645258353)
XLA Ops:
  0.6 0.0 copy-start.3
  0.6 0.0 copy-start
  0.7 0.0 copy-start.4
  0.7 0.0 copy-start.2
  0.7 0.0 copy-start.1
  1.4 0.0 copy-start.5
  1.4 0.0 copy-start.6
  1.4 3.4 %contribute.1 = bf16[1536,128]{1,0:T(8,128)(2,1)S(1)} custom-call(s32[1]{0:T(128)} %bitcast.place, s32[1]{0:T(128)S(6)} %copy.14.count, s32[128]{0:T(128)} %band_in.1, s32[128]{0:T(128)} %target_in.1, bf16[80,2048]{1,0:T(8,128)(2,1)} %cot_in.1, bf16[128,128,128]{2,1,0:T(8,128)(2,1)} %weight_in.1), custom_call_target="tpu_custom_call" | custom-call | tf_op jit(solution)/shard_map/contribute/pallas_call | solution.py:217
  4.9 26.6 %all_to_all.20 = bf16[64,24,128]{2,1,0:T(8,128)(2,1)S(1)} all-to-all(bf16[64,24,128]{2,1,0:T(8,128)(2,1)S(1)} %bitcast.6), channel_id=1, replica_groups=mesh['chan'=8,'y'=8,'x'=4,'core'=2] {'y','x','core'}, dimensions={0} | all-to-all | bytes 786432 | tf_op jit(solution)/shard_map/all_to_all | solution.py:234
  31.4 0.0 copy-done.3
  31.4 0.0 copy-done
  31.4 0.0 copy-done.4
  31.4 0.6 collect.1
  32.0 22.6 %all_to_all.21 = bf16[8,160,128]{2,1,0:T(8,128)(2,1)S(1)} all-to-all(bf16[8,160,128]{2,1,0:T(8,128)(2,1)S(1)} %collect.1), channel_id=1, replica_groups=mesh['chan'=8,'y'=8,'x'=4,'core'=2] {'chan'}, dimensions={0} | all-to-all | bytes 655360 | tf_op jit(solution)/shard_map/all_to_all | solution.py:241
  54.6 0.0 copy-done.2
  54.6 0.0 copy-done.1
  54.6 0.8 %weight_share.1 = f32[8,40,128]{2,1,0:T(8,128)S(1)} custom-call(bf16[1280,128]{1,0:T(8,128)(2,1)S(1)} %bitcast.4, bf16[64,2048]{1,0:T(8,128)(2,1)S(1)} %copy-done.1, f32[256,128]{1,0:T(8,128)S(1)} %copy-done.2), custom_call_target="tpu_custom_call" | custom-call | tf_op jit(solution)/shard_map/weight_share/pallas_call | solution.py:243
  55.4 10.2 %all_to_all.22.got = f32[8,40,128]{2,1,0:T(8,128)S(1)} all-to-all(f32[8,40,128]{2,1,0:T(8,128)S(1)} %weight_share.1), channel_id=1, replica_groups=mesh['chan'=8,'y'=8,'x'=4,'core'=2] {'x','core'}, dimensions={0} | all-to-all | bytes 327680 | tf_op jit(solution)/shard_map/all_to_all | solution.py:250
  65.6 0.7 add_copies.1
  66.3 3.4 %all-to-all-start.3 = ((f32[8,40,128]{2,1,0:T(8,128)}), f32[8,40,128]{2,1,0:T(8,128)S(1)}, u32[]{:S(2)}, u32[]{:S(2)}) async-start(f32[8,40,128]{2,1,0:T(8,128)} %add_copies.1), calls=%async_computation.3 | async-start | bytes 327680 | tf_op jit(solution)/shard_map/all_to_all | solution.py:264
  69.7 0.0 copy-done.5
  69.7 0.0 copy-done.6
  69.7 1.1 %feature_part.1 = bf16[64,2048]{1,0:T(8,128)(2,1)} custom-call(bf16[1280,128]{1,0:T(8,128)(2,1)S(1)} %bitcast.5, bf16[64,80]{1,0:T(8,128)(2,1)S(1)} %copy-done.6, bf16[80,256]{1,0:T(8,128)(2,1)S(1)} %copy-done.5), custom_call_target="tpu_custom_call" | custom-call | tf_op jit(solution)/shard_map/feature_part/pallas_call | solution.py:251
  70.8 7.0 %all-to-all-done.3.got = f32[8,40,128]{2,1,0:T(8,128)S(1)} async-done(((f32[8,40,128]{2,1,0:T(8,128)}), f32[8,40,128]{2,1,0:T(8,128)S(1)}, u32[]{:S(2)}, u32[]{:S(2)}) %all-to-all-start.3) | async-done | bytes 163872 | tf_op jit(solution)/shard_map/all_to_all | solution.py:264
  77.9 0.7 add_last.1
Async XLA Ops:
  0.6 30.8 %copy-start.3 = (f32[8,1536]{1,0:T(8,128)S(1)}, f32[8,1536]{1,0:T(8,128)}, u32[]{:S(2)}) copy-start(f32[8,1536]{1,0:T(8,128)} %constant.34.clone.coef) | copy-start | bytes 147460
  0.6 30.8 %copy-start = (bf16[128,1536]{1,0:T(8,128)(2,1)S(1)}, bf16[128,1536]{1,0:T(8,128)(2,1)}, u32[]{:S(2)}) copy-start(bf16[128,1536]{1,0:T(8,128)(2,1)} %constant.33.clone.spread) | copy-start | bytes 1179652
  0.7 30.8 %copy-start.4 = (bf16[16,1536]{1,0:T(8,128)(2,1)S(1)}, bf16[16,1536]{1,0:T(8,128)(2,1)}, u32[]{:S(2)}) copy-start(bf16[16,1536]{1,0:T(8,128)(2,1)} %constant.32.clone.tag_pick) | copy-start | bytes 147460
  0.7 54.0 %copy-start.2 = (f32[256,128]{1,0:T(8,128)S(1)}, f32[256,128]{1,0:T(8,128)}, u32[]{:S(2)}) copy-start(f32[256,128]{1,0:T(8,128)} %constant.35.clone.fold) | copy-start | bytes 393220
  0.7 53.9 %copy-start.1 = (bf16[64,2048]{1,0:T(8,128)(2,1)S(1)}, bf16[64,2048]{1,0:T(8,128)(2,1)}, u32[]{:S(2)}) copy-start(bf16[64,2048]{1,0:T(8,128)(2,1)} %features.1) | copy-start | bytes 786436
  1.4 68.3 %copy-start.5 = (bf16[80,256]{1,0:T(8,128)(2,1)S(1)}, bf16[80,256]{1,0:T(8,128)(2,1)}, u32[]{:S(2)}) copy-start(bf16[80,256]{1,0:T(8,128)(2,1)} %constant.36.clone.proj) | copy-start | bytes 122884
  1.4 68.3 %copy-start.6 = (bf16[64,80]{1,0:T(8,128)(2,1)S(1)}, bf16[64,80]{1,0:T(8,128)(2,1)}, u32[]{:S(2)}) copy-start(bf16[64,80]{1,0:T(8,128)(2,1)} %head.1) | copy-start | bytes 30724
  66.3 11.6 %all-to-all-start.3 = ((f32[8,40,128]{2,1,0:T(8,128)}), f32[8,40,128]{2,1,0:T(8,128)S(1)}, u32[]{:S(2)}, u32[]{:S(2)}) async-start(f32[8,40,128]{2,1,0:T(8,128)} %add_copies.1), calls=%async_computation.3 | async-start | bytes 327680 | tf_op jit(solution)/shard_map/all_to_all | solution.py:264

commit v3 on v2

--- a/solution.py
+++ b/solution.py
@@ -17,7 +17,7 @@
 BLOCKS = 16
 OWN = VARS // NCHAN
 MSG = 24
-CHUNK = 16
+CHUNK = 32
 PART = OWN * BLOCKS
 GROUP = 8
 SPACE = ("y", "x", "core")
@@ -26,7 +26,8 @@
 
 
 def contribute(
-    place, count, band_in, target_in, cot_in, weight_in, out, band, target, cot, weight, lhs, acc, seen, sems,
+    place, count, band_in, target_in, cot_in, weight_in, out,
+    band, target, cot, weight, lhs, acc, seen, sems,
 ):
     chunks = SLOTS // CHUNK
     small = [
@@ -35,20 +36,19 @@
             ((cot_in, cot), (band_in, band), (target_in, target))
         )
     ]
-    parts = [
-        pltpu.make_async_copy(
-            weight_in.at[pl.ds(k * CHUNK, CHUNK)], weight.at[pl.ds(k * CHUNK, CHUNK)], sems.at[k]
-        )
-        for k in range(chunks)
-    ]
+
+    def part(k):
+        at = pl.ds(pl.multiple_of(k * CHUNK, CHUNK), CHUNK)
+        return pltpu.make_async_copy(weight_in.at[at], weight.at[at], sems.at[k])
+
     for copy in small:
         copy.start()
-    for copy in parts:
-        copy.start()
+    for k in range(chunks):
+        part(k).start()
     mine = place[0] // NSPACE
     space = place[0] % NSPACE
     for j in range(NSPACE):
-        seen[j] = 0
+        seen[j] = 2 * j
     row = lax.broadcasted_iota(jnp.int32, (32, VARS), 0)
     col = lax.broadcasted_iota(jnp.int32, (32, VARS), 1)
     low = row & 15
@@ -57,7 +57,9 @@
     pick = jnp.where(col == var + mine * OWN, 1.0, 0.0).astype(BF16)
     tag_row = lax.broadcasted_iota(jnp.int32, (8, B), 0)
     tag_lane = lax.broadcasted_iota(jnp.int32, (8, B), 1)
-    tag_lane = jnp.where(tag_row == 4, tag_lane, -1)
+    tag_lane = jnp.where(tag_row == 4, tag_lane - 2 * space, -1)
+    dead = 2 * BLOCKS
+    lhs[dead] = jnp.zeros((16, B), BF16)
     small[0].wait()
     rows = jnp.dot(pick, cot[...], preferred_element_type=F32).astype(BF16)
     for j in range(BLOCKS):
@@ -65,24 +67,23 @@
             lhs[2 * j + rank] = rows[16 * rank : 16 * rank + 16, j * B : (j + 1) * B]
     for copy in small[1:]:
         copy.wait()
+    live_slots = count[0]
 
     def chunk(k, carry):
-        base = k * CHUNK
-        pltpu.make_async_copy(
-            weight_in.at[pl.ds(base, CHUNK)], weight.at[pl.ds(base, CHUNK)], sems.at[k]
-        ).wait()
+        part(k).wait()
         for i in range(CHUNK):
-            slot = base + i
-            dest = target[slot] >> 4
-            rank = seen[dest]
-            seen[dest] = rank + 1
-            live = slot < count[0]
-            value = jnp.dot(lhs[2 * band[slot] + rank], weight[slot], preferred_element_type=F32)
-            value = jnp.where(live, value, 0.0)
-            tag = jnp.where(live, (target[slot] & 15) + 1, 0).astype(F32)
-            extra = value[8:16] + jnp.where(tag_lane == 2 * space + rank, tag, 0.0)
-            acc[dest, pl.ds(pl.multiple_of(8 * rank, 8), 8), :] = value[0:8]
-            acc[dest, pl.ds(pl.multiple_of(16 + 8 * rank, 8), 8), :] = extra
+            slot = k * CHUNK + i
+            goal = target[slot]
+            dest = goal >> 4
+            key = seen[dest]
+            seen[dest] = key + 1
+            rank = key & 1
+            live = slot < live_slots
+            source = jnp.where(live, 2 * band[slot] + rank, dead)
+            tag = jnp.where(live, (goal & 15) + 1, 0)
+            value = jnp.dot(lhs[source], weight[slot], preferred_element_type=F32)
+            acc[key, 0:8, :] = value[0:8]
+            acc[key, 8:16, :] = value[8:16] + jnp.where(tag_lane == rank, tag, 0).astype(F32)
         return carry
 
     lax.fori_loop(0, chunks, chunk, 0)
@@ -90,8 +91,8 @@
     def emit(k, carry):
         parts = []
         for half in range(2):
-            x = acc[2 * k + half]
-            parts += [x[0:16], x[16:24] + x[24:32]]
+            first, second = acc[4 * k + 2 * half], acc[4 * k + 2 * half + 1]
+            parts += [first[0:8], second[0:8], first[8:16] + second[8:16]]
         rows = jnp.concatenate(parts, axis=0).astype(BF16)
         out[pl.ds(pl.multiple_of(2 * MSG * k, 2 * MSG), 2 * MSG), :] = rows
         return carry
@@ -223,8 +224,8 @@
             pltpu.SMEM((SLOTS,), jnp.int32),
             pltpu.VMEM((VARS, BLOCKS * B), BF16),
             pltpu.VMEM((SLOTS, B, B), BF16),
-            pltpu.VMEM((2 * BLOCKS, 16, B), BF16),
-            pltpu.VMEM((NSPACE, 32, B), F32),
+            pltpu.VMEM((2 * BLOCKS + 1, 16, B), BF16),
+            pltpu.VMEM((SLOTS, 16, B), F32),
             pltpu.SMEM((NSPACE,), jnp.int32),
             pltpu.SemaphoreType.DMA((SLOTS // CHUNK + 3,)),
         ],

time: 78.9 us -> 78.6 us (level)
  no operation moved by 1% of the time
where the time goes in v3:
time: 78.6 us; the launch traced here: 78.2 us
  blocking collectives  59.4 us (76%)
  waiting for transfers between devices  7.05 us (9%)
  Pallas kernels  6.91 us (9%)
  starting transfers between devices  3.38 us (4%)
  between operations  1.47 us (2%)
    all_to_all x1, blocking collectives, on_device(): got = lax.all_to_all(sent.reshape(NSPACE, MSG, B), SPACE, 0, 0, tiled=True)  26.6 us
    all_to_all x1, blocking collectives, on_device(): lax.all_to_all(parts, 'chan', 0, 0, tiled=True).reshape(NCHAN * PART, B)  22.6 us
    all_to_all x1, blocking collectives, on_device(): share = lax.all_to_all(share, ('x', 'core'), 0, 0, tiled=True)  10.2 us
    all_to_all x1, waiting for transfers between devices, on_device(): share = lax.all_to_all(share, 'y', 0, 0, tiled=True)  7.05 us
    all_to_all x1, starting transfers between devices, on_device(): share = lax.all_to_all(share, 'y', 0, 0, tiled=True)  3.38 us
    pallas_call x1, Pallas kernels, on_device(): pl.pallas_call(contribute, out_shape=jax.ShapeDtypeStruct((NSPACE * MSG,...  3.05 us
  transfers between devices with their start and end apart: 1, of which 1 were waited for; matrix products, arithmetic and copies ran while one was open for 0% of the time, Pallas kernels for 1%

profile of v3, /device:TPU:1, one launch (start us, length us, event | category | flops | bytes accessed | tf_op | source)
XLA Modules:
  0.0 78.2 jit_solution(11750251854854743716)
XLA Ops:
  0.6 0.0 copy-start.3
  0.6 0.0 copy-start
  0.7 0.0 copy-start.4
  0.7 0.0 copy-start.2
  0.7 0.0 copy-start.1
  1.4 0.0 copy-start.5
  1.4 0.0 copy-start.6
  1.4 3.1 %contribute.1 = bf16[1536,128]{1,0:T(8,128)(2,1)S(1)} custom-call(s32[1]{0:T(128)} %bitcast.place, s32[1]{0:T(128)S(6)} %copy.14.count, s32[128]{0:T(128)} %band_in.1, s32[128]{0:T(128)} %target_in.1, bf16[80,2048]{1,0:T(8,128)(2,1)} %cot_in.1, bf16[128,128,128]{2,1,0:T(8,128)(2,1)} %weight_in.1), custom_call_target="tpu_custom_call" | custom-call | tf_op jit(solution)/shard_map/contribute/pallas_call | solution.py:218
  4.5 26.6 %all_to_all.20 = bf16[64,24,128]{2,1,0:T(8,128)(2,1)S(1)} all-to-all(bf16[64,24,128]{2,1,0:T(8,128)(2,1)S(1)} %bitcast.6), channel_id=1, replica_groups=mesh['chan'=8,'y'=8,'x'=4,'core'=2] {'y','x','core'}, dimensions={0} | all-to-all | bytes 786432 | tf_op jit(solution)/shard_map/all_to_all | solution.py:235
  31.1 0.0 copy-done.3
  31.1 0.0 copy-done
  31.1 0.0 copy-done.4
  31.1 0.6 collect.1
  31.6 22.6 %all_to_all.21 = bf16[8,160,128]{2,1,0:T(8,128)(2,1)S(1)} all-to-all(bf16[8,160,128]{2,1,0:T(8,128)(2,1)S(1)} %collect.1), channel_id=1, replica_groups=mesh['chan'=8,'y'=8,'x'=4,'core'=2] {'chan'}, dimensions={0} | all-to-all | bytes 655360 | tf_op jit(solution)/shard_map/all_to_all | solution.py:242
  54.3 0.0 copy-done.2
  54.3 0.0 copy-done.1
  54.3 0.8 %weight_share.1 = f32[8,40,128]{2,1,0:T(8,128)S(1)} custom-call(bf16[1280,128]{1,0:T(8,128)(2,1)S(1)} %bitcast.4, bf16[64,2048]{1,0:T(8,128)(2,1)S(1)} %copy-done.1, f32[256,128]{1,0:T(8,128)S(1)} %copy-done.2), custom_call_target="tpu_custom_call" | custom-call | tf_op jit(solution)/shard_map/weight_share/pallas_call | solution.py:244
  55.1 10.2 %all_to_all.22.got = f32[8,40,128]{2,1,0:T(8,128)S(1)} all-to-all(f32[8,40,128]{2,1,0:T(8,128)S(1)} %weight_share.1), channel_id=1, replica_groups=mesh['chan'=8,'y'=8,'x'=4,'core'=2] {'x','core'}, dimensions={0} | all-to-all | bytes 327680 | tf_op jit(solution)/shard_map/all_to_all | solution.py:251
  65.3 0.7 add_copies.1
  65.9 3.4 %all-to-all-start.3 = ((f32[8,40,128]{2,1,0:T(8,128)}), f32[8,40,128]{2,1,0:T(8,128)S(1)}, u32[]{:S(2)}, u32[]{:S(2)}) async-start(f32[8,40,128]{2,1,0:T(8,128)} %add_copies.1), calls=%async_computation.3 | async-start | bytes 327680 | tf_op jit(solution)/shard_map/all_to_all | solution.py:265
  69.3 0.0 copy-done.5
  69.3 0.0 copy-done.6
  69.4 1.1 %feature_part.1 = bf16[64,2048]{1,0:T(8,128)(2,1)} custom-call(bf16[1280,128]{1,0:T(8,128)(2,1)S(1)} %bitcast.5, bf16[64,80]{1,0:T(8,128)(2,1)S(1)} %copy-done.6, bf16[80,256]{1,0:T(8,128)(2,1)S(1)} %copy-done.5), custom_call_target="tpu_custom_call" | custom-call | tf_op jit(solution)/shard_map/feature_part/pallas_call | solution.py:252
  70.5 7.0 %all-to-all-done.3.got = f32[8,40,128]{2,1,0:T(8,128)S(1)} async-done(((f32[8,40,128]{2,1,0:T(8,128)}), f32[8,40,128]{2,1,0:T(8,128)S(1)}, u32[]{:S(2)}, u32[]{:S(2)}) %all-to-all-start.3) | async-done | bytes 163872 | tf_op jit(solution)/shard_map/all_to_all | solution.py:265
  77.5 0.7 add_last.1
Async XLA Ops:
  0.6 30.4 %copy-start.3 = (f32[8,1536]{1,0:T(8,128)S(1)}, f32[8,1536]{1,0:T(8,128)}, u32[]{:S(2)}) copy-start(f32[8,1536]{1,0:T(8,128)} %constant.34.clone.coef) | copy-start | bytes 147460
  0.6 30.4 %copy-start = (bf16[128,1536]{1,0:T(8,128)(2,1)S(1)}, bf16[128,1536]{1,0:T(8,128)(2,1)}, u32[]{:S(2)}) copy-start(bf16[128,1536]{1,0:T(8,128)(2,1)} %constant.33.clone.spread) | copy-start | bytes 1179652
  0.7 30.4 %copy-start.4 = (bf16[16,1536]{1,0:T(8,128)(2,1)S(1)}, bf16[16,1536]{1,0:T(8,128)(2,1)}, u32[]{:S(2)}) copy-start(bf16[16,1536]{1,0:T(8,128)(2,1)} %constant.32.clone.tag_pick) | copy-start | bytes 147460
  0.7 53.6 %copy-start.2 = (f32[256,128]{1,0:T(8,128)S(1)}, f32[256,128]{1,0:T(8,128)}, u32[]{:S(2)}) copy-start(f32[256,128]{1,0:T(8,128)} %constant.35.clone.fold) | copy-start | bytes 393220
  0.7 53.6 %copy-start.1 = (bf16[64,2048]{1,0:T(8,128)(2,1)S(1)}, bf16[64,2048]{1,0:T(8,128)(2,1)}, u32[]{:S(2)}) copy-start(bf16[64,2048]{1,0:T(8,128)(2,1)} %features.1) | copy-start | bytes 786436
  1.4 67.9 %copy-start.5 = (bf16[80,256]{1,0:T(8,128)(2,1)S(1)}, bf16[80,256]{1,0:T(8,128)(2,1)}, u32[]{:S(2)}) copy-start(bf16[80,256]{1,0:T(8,128)(2,1)} %constant.36.clone.proj) | copy-start | bytes 122884
  1.4 67.9 %copy-start.6 = (bf16[64,80]{1,0:T(8,128)(2,1)S(1)}, bf16[64,80]{1,0:T(8,128)(2,1)}, u32[]{:S(2)}) copy-start(bf16[64,80]{1,0:T(8,128)(2,1)} %head.1) | copy-start | bytes 30724
  65.9 11.6 %all-to-all-start.3 = ((f32[8,40,128]{2,1,0:T(8,128)}), f32[8,40,128]{2,1,0:T(8,128)S(1)}, u32[]{:S(2)}, u32[]{:S(2)}) async-start(f32[8,40,128]{2,1,0:T(8,128)} %add_copies.1), calls=%async_computation.3 | async-start | bytes 327680 | tf_op jit(solution)/shard_map/all_to_all | solution.py:265

commit v4 on v3

--- a/solution.py
+++ b/solution.py
@@ -43,8 +43,14 @@
 
     for copy in small:
         copy.start()
+    live_slots = count[0]
+    groups = (live_slots + (CHUNK - 1)) // CHUNK
     for k in range(chunks):
-        part(k).start()
+
+        @pl.when(k < groups)
+        def _():
+            part(k).start()
+
     mine = place[0] // NSPACE
     space = place[0] % NSPACE
     for j in range(NSPACE):
@@ -60,6 +66,7 @@
     tag_lane = jnp.where(tag_row == 4, tag_lane - 2 * space, -1)
     dead = 2 * BLOCKS
     lhs[dead] = jnp.zeros((16, B), BF16)
+    acc[...] = jnp.zeros_like(acc)
     small[0].wait()
     rows = jnp.dot(pick, cot[...], preferred_element_type=F32).astype(BF16)
     for j in range(BLOCKS):
@@ -67,7 +74,6 @@
             lhs[2 * j + rank] = rows[16 * rank : 16 * rank + 16, j * B : (j + 1) * B]
     for copy in small[1:]:
         copy.wait()
-    live_slots = count[0]
 
     def chunk(k, carry):
         part(k).wait()
@@ -86,7 +92,7 @@
             acc[key, 8:16, :] = value[8:16] + jnp.where(tag_lane == rank, tag, 0).astype(F32)
         return carry
 
-    lax.fori_loop(0, chunks, chunk, 0)
+    lax.fori_loop(0, groups, chunk, 0)
 
     def emit(k, carry):
         parts = []

time: 78.6 us -> 77.4 us (0.985)
  blocking collectives: 59.4 us -> 58.2 us
    all_to_all x1, blocking collectives: 26.6 us -> 25.4 us  [on_device(): got = lax.all_to_all(sent.reshape(NSPACE, MSG, B), SPACE, 0, 0, tiled=True)]
where the time goes in v4:
time: 77.4 us; the launch traced here: 77.1 us
  blocking collectives  58.2 us (75%)
  waiting for transfers between devices  7.05 us (9%)
  Pallas kernels  6.91 us (9%)
  starting transfers between devices  3.38 us (4%)
  between operations  1.47 us (2%)
    all_to_all x1, blocking collectives, on_device(): got = lax.all_to_all(sent.reshape(NSPACE, MSG, B), SPACE, 0, 0, tiled=True)  25.4 us
    all_to_all x1, blocking collectives, on_device(): lax.all_to_all(parts, 'chan', 0, 0, tiled=True).reshape(NCHAN * PART, B)  22.6 us
    all_to_all x1, blocking collectives, on_device(): share = lax.all_to_all(share, ('x', 'core'), 0, 0, tiled=True)  10.2 us
    all_to_all x1, waiting for transfers between devices, on_device(): share = lax.all_to_all(share, 'y', 0, 0, tiled=True)  7.05 us
    all_to_all x1, starting transfers between devices, on_device(): share = lax.all_to_all(share, 'y', 0, 0, tiled=True)  3.38 us
    pallas_call x1, Pallas kernels, on_device(): pl.pallas_call(contribute, out_shape=jax.ShapeDtypeStruct((NSPACE * MSG,...  3.06 us
  transfers between devices with their start and end apart: 1, of which 1 were waited for; matrix products, arithmetic and copies ran while one was open for 0% of the time, Pallas kernels for 1%

profile of v4, /device:TPU:1, one launch (start us, length us, event | category | flops | bytes accessed | tf_op | source)
XLA Modules:
  0.0 77.1 jit_solution(8631262655206059422)
XLA Ops:
  0.6 0.0 copy-start.3
  0.6 0.0 copy-start
  0.7 0.0 copy-start.4
  0.7 0.0 copy-start.2
  0.7 0.0 copy-start.1
  1.4 0.0 copy-start.5
  1.4 0.0 copy-start.6
  1.4 3.1 %contribute.1 = bf16[1536,128]{1,0:T(8,128)(2,1)S(1)} custom-call(s32[1]{0:T(128)} %bitcast.place, s32[1]{0:T(128)S(6)} %copy.14.count, s32[128]{0:T(128)} %band_in.1, s32[128]{0:T(128)} %target_in.1, bf16[80,2048]{1,0:T(8,128)(2,1)} %cot_in.1, bf16[128,128,128]{2,1,0:T(8,128)(2,1)} %weight_in.1), custom_call_target="tpu_custom_call" | custom-call | tf_op jit(solution)/shard_map/contribute/pallas_call | solution.py:224
  4.5 25.4 %all_to_all.20 = bf16[64,24,128]{2,1,0:T(8,128)(2,1)S(1)} all-to-all(bf16[64,24,128]{2,1,0:T(8,128)(2,1)S(1)} %bitcast.6), channel_id=1, replica_groups=mesh['chan'=8,'y'=8,'x'=4,'core'=2] {'y','x','core'}, dimensions={0} | all-to-all | bytes 786432 | tf_op jit(solution)/shard_map/all_to_all | solution.py:241
  29.9 0.0 copy-done.3
  29.9 0.0 copy-done
  29.9 0.0 copy-done.4
  29.9 0.6 collect.1
  30.5 22.6 %all_to_all.21 = bf16[8,160,128]{2,1,0:T(8,128)(2,1)S(1)} all-to-all(bf16[8,160,128]{2,1,0:T(8,128)(2,1)S(1)} %collect.1), channel_id=1, replica_groups=mesh['chan'=8,'y'=8,'x'=4,'core'=2] {'chan'}, dimensions={0} | all-to-all | bytes 655360 | tf_op jit(solution)/shard_map/all_to_all | solution.py:248
  53.1 0.0 copy-done.2
  53.1 0.0 copy-done.1
  53.1 0.8 %weight_share.1 = f32[8,40,128]{2,1,0:T(8,128)S(1)} custom-call(bf16[1280,128]{1,0:T(8,128)(2,1)S(1)} %bitcast.4, bf16[64,2048]{1,0:T(8,128)(2,1)S(1)} %copy-done.1, f32[256,128]{1,0:T(8,128)S(1)} %copy-done.2), custom_call_target="tpu_custom_call" | custom-call | tf_op jit(solution)/shard_map/weight_share/pallas_call | solution.py:250
  53.9 10.2 %all_to_all.22.got = f32[8,40,128]{2,1,0:T(8,128)S(1)} all-to-all(f32[8,40,128]{2,1,0:T(8,128)S(1)} %weight_share.1), channel_id=1, replica_groups=mesh['chan'=8,'y'=8,'x'=4,'core'=2] {'x','core'}, dimensions={0} | all-to-all | bytes 327680 | tf_op jit(solution)/shard_map/all_to_all | solution.py:257
  64.1 0.7 add_copies.1
  64.8 3.4 %all-to-all-start.3 = ((f32[8,40,128]{2,1,0:T(8,128)}), f32[8,40,128]{2,1,0:T(8,128)S(1)}, u32[]{:S(2)}, u32[]{:S(2)}) async-start(f32[8,40,128]{2,1,0:T(8,128)} %add_copies.1), calls=%async_computation.3 | async-start | bytes 327680 | tf_op jit(solution)/shard_map/all_to_all | solution.py:271
  68.2 0.0 copy-done.5
  68.2 0.0 copy-done.6
  68.2 1.1 %feature_part.1 = bf16[64,2048]{1,0:T(8,128)(2,1)} custom-call(bf16[1280,128]{1,0:T(8,128)(2,1)S(1)} %bitcast.5, bf16[64,80]{1,0:T(8,128)(2,1)S(1)} %copy-done.6, bf16[80,256]{1,0:T(8,128)(2,1)S(1)} %copy-done.5), custom_call_target="tpu_custom_call" | custom-call | tf_op jit(solution)/shard_map/feature_part/pallas_call | solution.py:258
  69.3 7.1 %all-to-all-done.3.got = f32[8,40,128]{2,1,0:T(8,128)S(1)} async-done(((f32[8,40,128]{2,1,0:T(8,128)}), f32[8,40,128]{2,1,0:T(8,128)S(1)}, u32[]{:S(2)}, u32[]{:S(2)}) %all-to-all-start.3) | async-done | bytes 163872 | tf_op jit(solution)/shard_map/all_to_all | solution.py:271
  76.4 0.7 add_last.1
Async XLA Ops:
  0.6 29.3 %copy-start.3 = (f32[8,1536]{1,0:T(8,128)S(1)}, f32[8,1536]{1,0:T(8,128)}, u32[]{:S(2)}) copy-start(f32[8,1536]{1,0:T(8,128)} %constant.34.clone.coef) | copy-start | bytes 147460
  0.6 29.3 %copy-start = (bf16[128,1536]{1,0:T(8,128)(2,1)S(1)}, bf16[128,1536]{1,0:T(8,128)(2,1)}, u32[]{:S(2)}) copy-start(bf16[128,1536]{1,0:T(8,128)(2,1)} %constant.33.clone.spread) | copy-start | bytes 1179652
  0.7 29.2 %copy-start.4 = (bf16[16,1536]{1,0:T(8,128)(2,1)S(1)}, bf16[16,1536]{1,0:T(8,128)(2,1)}, u32[]{:S(2)}) copy-start(bf16[16,1536]{1,0:T(8,128)(2,1)} %constant.32.clone.tag_pick) | copy-start | bytes 147460
  0.7 52.4 %copy-start.2 = (f32[256,128]{1,0:T(8,128)S(1)}, f32[256,128]{1,0:T(8,128)}, u32[]{:S(2)}) copy-start(f32[256,128]{1,0:T(8,128)} %constant.35.clone.fold) | copy-start | bytes 393220
  0.7 52.4 %copy-start.1 = (bf16[64,2048]{1,0:T(8,128)(2,1)S(1)}, bf16[64,2048]{1,0:T(8,128)(2,1)}, u32[]{:S(2)}) copy-start(bf16[64,2048]{1,0:T(8,128)(2,1)} %features.1) | copy-start | bytes 786436
  1.4 66.8 %copy-start.5 = (bf16[80,256]{1,0:T(8,128)(2,1)S(1)}, bf16[80,256]{1,0:T(8,128)(2,1)}, u32[]{:S(2)}) copy-start(bf16[80,256]{1,0:T(8,128)(2,1)} %constant.36.clone.proj) | copy-start | bytes 122884
  1.4 66.7 %copy-start.6 = (bf16[64,80]{1,0:T(8,128)(2,1)S(1)}, bf16[64,80]{1,0:T(8,128)(2,1)}, u32[]{:S(2)}) copy-start(bf16[64,80]{1,0:T(8,128)(2,1)} %head.1) | copy-start | bytes 30724
  64.8 11.6 %all-to-all-start.3 = ((f32[8,40,128]{2,1,0:T(8,128)}), f32[8,40,128]{2,1,0:T(8,128)S(1)}, u32[]{:S(2)}, u32[]{:S(2)}) async-start(f32[8,40,128]{2,1,0:T(8,128)} %add_copies.1), calls=%async_computation.3 | async-start | bytes 327680 | tf_op jit(solution)/shard_map/all_to_all | solution.py:271

commit v5 on v4

--- a/solution.py
+++ b/solution.py
@@ -132,8 +132,12 @@
             )
 
 
-def weight_share(parts, features, fold, share, wide):
+def heads(parts, features, head, proj, fold, grad_out, share, wide, grad, sem):
     widen(parts, wide)
+    lifted = jnp.dot(head[...], proj[...], preferred_element_type=F32).astype(BF16)
+    grad[...] = jnp.dot(lifted, wide[...], preferred_element_type=F32).astype(BF16)
+    copy = pltpu.make_async_copy(grad, grad_out, sem)
+    copy.start()
     total = lax.dot_general(
         features[...], wide[...], (((1,), (1,)), ((), ())), preferred_element_type=F32
     )
@@ -149,12 +153,7 @@
     for j in range(GROUP):
         share[j, 0:32] = front
         share[j, 32:40] = back
-
-
-def feature_part(parts, head, proj, grad, wide):
-    widen(parts, wide)
-    lifted = jnp.dot(head[...], proj[...], preferred_element_type=F32).astype(BF16)
-    grad[...] = jnp.dot(lifted, wide[...], preferred_element_type=F32).astype(BF16)
+    copy.wait()
 
 
 def add_up(got):
@@ -247,21 +246,22 @@
     )(near(got.reshape(NSPACE * MSG, B)), tag_pick, spread, coef)
     parts = lax.all_to_all(parts, "chan", 0, 0, tiled=True).reshape(NCHAN * PART, B)
     parts = near(parts)
-    share = pl.pallas_call(
-        weight_share,
-        out_shape=jax.ShapeDtypeStruct((GROUP, 40, B), F32),
-        scratch_shapes=[pltpu.VMEM((256, hp_local), BF16)],
+    feature_grad, share = pl.pallas_call(
+        heads,
+        out_shape=(
+            jax.ShapeDtypeStruct((head_weight.shape[0], hp_local), BF16),
+            jax.ShapeDtypeStruct((GROUP, 40, B), F32),
+        ),
+        out_specs=(hbm, pl.BlockSpec(memory_space=pltpu.VMEM)),
+        scratch_shapes=[
+            pltpu.VMEM((256, hp_local), BF16),
+            pltpu.VMEM((head_weight.shape[0], hp_local), BF16),
+            pltpu.SemaphoreType.DMA(()),
+        ],
         compiler_params=small_grant(8),
-        name="weight_share",
-    )(parts, features, fold)
+        name="heads",
+    )(parts, features, head_weight, proj, fold)
     share = lax.all_to_all(share, ("x", "core"), 0, 0, tiled=True)
-    feature_grad = pl.pallas_call(
-        feature_part,
-        out_shape=jax.ShapeDtypeStruct((head_weight.shape[0], hp_local), BF16),
-        scratch_shapes=[pltpu.VMEM((256, hp_local), BF16)],
-        compiler_params=small_grant(8),
-        name="feature_part",
-    )(parts, head_weight, proj)
     share = pl.pallas_call(
         add_copies,
         out_shape=jax.ShapeDtypeStruct(share.shape, F32),

time: 77.4 us -> 76.1 us (0.983)
  blocking collectives: 58.2 us -> 68.7 us
  waiting for transfers between devices: 7.05 us -> 0 us
  starting transfers between devices: 3.38 us -> 0 us
  Pallas kernels: 6.91 us -> 5.47 us
    all_to_all x0 -> x1, blocking collectives: none -> 10.5 us  [on_device(): share = lax.all_to_all(share, 'y', 0, 0, tiled=True)]
    all_to_all x1 -> x0, waiting for transfers between devices: 7.05 us -> none  [on_device(): share = lax.all_to_all(share, 'y', 0, 0, tiled=True)]
    all_to_all x1 -> x0, starting transfers between devices: 3.38 us -> none  [on_device(): share = lax.all_to_all(share, 'y', 0, 0, tiled=True)]
    pallas_call x2 -> x1, Pallas kernels: 1.93 us -> 1.14 us  [on_device(): pl.pallas_call(heads, out_shape=(jax.ShapeDtypeStruct((head_weight.shape[...]
  transfers between devices with their start and end apart: 1 -> 0, of which waited for: 1 -> 0; matrix products, arithmetic and copies ran while one was open for 0% -> 0% of each run, Pallas kernels for 1% -> 0%
where the time goes in v5:
time: 76.1 us; the launch traced here: 75.7 us
  blocking collectives  68.7 us (90%)
  Pallas kernels  5.47 us (7%)
  between operations  1.45 us (2%)
    all_to_all x1, blocking collectives, on_device(): got = lax.all_to_all(sent.reshape(NSPACE, MSG, B), SPACE, 0, 0, tiled=True)  25.4 us
    all_to_all x1, blocking collectives, on_device(): lax.all_to_all(parts, 'chan', 0, 0, tiled=True).reshape(NCHAN * PART, B)  22.6 us
    all_to_all x1, blocking collectives, on_device(): share = lax.all_to_all(share, 'y', 0, 0, tiled=True)  10.5 us
    all_to_all x1, blocking collectives, on_device(): share = lax.all_to_all(share, ('x', 'core'), 0, 0, tiled=True)  10.2 us
    pallas_call x1, Pallas kernels, on_device(): pl.pallas_call(contribute, out_shape=jax.ShapeDtypeStruct((NSPACE * MSG,...  3.05 us

profile of v5, /device:TPU:1, one launch (start us, length us, event | category | flops | bytes accessed | tf_op | source)
XLA Modules:
  0.0 75.7 jit_solution(4218973767166127574)
XLA Ops:
  0.6 0.0 copy-start.3
  0.6 0.0 copy-start
  0.7 0.0 copy-start.4
  0.7 0.0 copy-start.2
  0.7 0.0 copy-start.5
  0.7 0.0 copy-start.1
  0.7 0.0 copy-start.6
  1.4 3.0 %contribute.1 = bf16[1536,128]{1,0:T(8,128)(2,1)S(1)} custom-call(s32[1]{0:T(128)} %bitcast.place, s32[1]{0:T(128)S(6)} %copy.14.count, s32[128]{0:T(128)} %band_in.1, s32[128]{0:T(128)} %target_in.1, bf16[80,2048]{1,0:T(8,128)(2,1)} %cot_in.1, bf16[128,128,128]{2,1,0:T(8,128)(2,1)} %weight_in.1), custom_call_target="tpu_custom_call" | custom-call | tf_op jit(solution)/shard_map/contribute/pallas_call | solution.py:223
  4.5 25.4 %all_to_all.20 = bf16[64,24,128]{2,1,0:T(8,128)(2,1)S(1)} all-to-all(bf16[64,24,128]{2,1,0:T(8,128)(2,1)S(1)} %bitcast.4), channel_id=1, replica_groups=mesh['chan'=8,'y'=8,'x'=4,'core'=2] {'y','x','core'}, dimensions={0} | all-to-all | bytes 786432 | tf_op jit(solution)/shard_map/all_to_all | solution.py:240
  29.9 0.0 copy-done.3
  29.9 0.0 copy-done
  29.9 0.0 copy-done.4
  29.9 0.6 collect.1
  30.5 22.6 %all_to_all.21 = bf16[8,160,128]{2,1,0:T(8,128)(2,1)S(1)} all-to-all(bf16[8,160,128]{2,1,0:T(8,128)(2,1)S(1)} %collect.1), channel_id=1, replica_groups=mesh['chan'=8,'y'=8,'x'=4,'core'=2] {'chan'}, dimensions={0} | all-to-all | bytes 655360 | tf_op jit(solution)/shard_map/all_to_all | solution.py:247
  53.1 0.0 copy-done.2
  53.1 0.0 copy-done.5
  53.1 0.0 copy-done.1
  53.1 0.0 copy-done.6
  53.1 1.1 %heads.1 = (bf16[64,2048]{1,0:T(8,128)(2,1)}, f32[8,40,128]{2,1,0:T(8,128)S(1)}) custom-call(bf16[1280,128]{1,0:T(8,128)(2,1)S(1)} %bitcast.6, bf16[64,2048]{1,0:T(8,128)(2,1)S(1)} %copy-done.1, bf16[64,80]{1,0:T(8,128)(2,1)S(1)} %copy-done.6, bf16[80,256]{1,0:T(8,128)(2,1)S(1)} %copy-done.5, f32[256,128]{1,0:T(8,128)S(1)} %copy-done.2), custom_call_target="tpu_custom_call" | custom-call | tf_op jit(solution)/shard_map/heads/pallas_call | solution.py:249
  54.2 10.2 %all_to_all.22.got = f32[8,40,128]{2,1,0:T(8,128)S(1)} all-to-all(f32[8,40,128]{2,1,0:T(8,128)S(1)} %get-tuple-element.5), channel_id=1, replica_groups=mesh['chan'=8,'y'=8,'x'=4,'core'=2] {'x','core'}, dimensions={0} | all-to-all | bytes 327680 | tf_op jit(solution)/shard_map/all_to_all | solution.py:264
  64.5 10.5 %all_to_all.23.got = f32[8,40,128]{2,1,0:T(8,128)S(1)} all-to-all(f32[8,40,128]{2,1,0:T(8,128)S(1)} %add_copies.1), channel_id=1, replica_groups=mesh['chan'=8,'y'=8,'x'=4,'core'=2] {'y'}, dimensions={0} | all-to-all | bytes 327680 | tf_op jit(solution)/shard_map/all_to_all | solution.py:271
  75.0 0.7 add_last.1
  (1 shorter events, 0.0 us)
Async XLA Ops:
  0.6 29.3 %copy-start.3 = (f32[8,1536]{1,0:T(8,128)S(1)}, f32[8,1536]{1,0:T(8,128)}, u32[]{:S(2)}) copy-start(f32[8,1536]{1,0:T(8,128)} %constant.34.clone.coef) | copy-start | bytes 147460
  0.6 29.2 %copy-start = (bf16[128,1536]{1,0:T(8,128)(2,1)S(1)}, bf16[128,1536]{1,0:T(8,128)(2,1)}, u32[]{:S(2)}) copy-start(bf16[128,1536]{1,0:T(8,128)(2,1)} %constant.33.clone.spread) | copy-start | bytes 1179652
  0.7 29.2 %copy-start.4 = (bf16[16,1536]{1,0:T(8,128)(2,1)S(1)}, bf16[16,1536]{1,0:T(8,128)(2,1)}, u32[]{:S(2)}) copy-start(bf16[16,1536]{1,0:T(8,128)(2,1)} %constant.32.clone.tag_pick) | copy-start | bytes 147460
  0.7 52.4 %copy-start.2 = (f32[256,128]{1,0:T(8,128)S(1)}, f32[256,128]{1,0:T(8,128)}, u32[]{:S(2)}) copy-start(f32[256,128]{1,0:T(8,128)} %constant.36.clone.fold) | copy-start | bytes 393220
  0.7 52.4 %copy-start.5 = (bf16[80,256]{1,0:T(8,128)(2,1)S(1)}, bf16[80,256]{1,0:T(8,128)(2,1)}, u32[]{:S(2)}) copy-start(bf16[80,256]{1,0:T(8,128)(2,1)} %constant.35.clone.proj) | copy-start | bytes 122884
  0.7 52.4 %copy-start.1 = (bf16[64,2048]{1,0:T(8,128)(2,1)S(1)}, bf16[64,2048]{1,0:T(8,128)(2,1)}, u32[]{:S(2)}) copy-start(bf16[64,2048]{1,0:T(8,128)(2,1)} %features.1) | copy-start | bytes 786436
  0.7 52.4 %copy-start.6 = (bf16[64,80]{1,0:T(8,128)(2,1)S(1)}, bf16[64,80]{1,0:T(8,128)(2,1)}, u32[]{:S(2)}) copy-start(bf16[64,80]{1,0:T(8,128)(2,1)} %head.1) | copy-start | bytes 30724

commit v6 on v5

--- a/solution.py
+++ b/solution.py
@@ -16,7 +16,7 @@
 SLOTS = 128
 BLOCKS = 16
 OWN = VARS // NCHAN
-MSG = 24
+MSG = 22
 CHUNK = 32
 PART = OWN * BLOCKS
 GROUP = 8
@@ -94,24 +94,47 @@
 
     lax.fori_loop(0, groups, chunk, 0)
 
+    sub = lax.broadcasted_iota(jnp.int32, (8, B), 0)
+
     def emit(k, carry):
-        parts = []
-        for half in range(2):
-            first, second = acc[4 * k + 2 * half], acc[4 * k + 2 * half + 1]
-            parts += [first[0:8], second[0:8], first[8:16] + second[8:16]]
-        rows = jnp.concatenate(parts, axis=0).astype(BF16)
-        out[pl.ds(pl.multiple_of(2 * MSG * k, 2 * MSG), 2 * MSG), :] = rows
+        tiles = []
+        for quad in range(2):
+            first, second, extra, turned = [], [], [], []
+            for h in range(4):
+                one, two = acc[16 * k + 8 * quad + 2 * h], acc[16 * k + 8 * quad + 2 * h + 1]
+                first.append(one[0:8])
+                second.append(two[0:8])
+                extra.append(one[8:16] + two[8:16])
+                turned.append(pltpu.roll(extra[h], 2, 0))
+            for h in range(4):
+                tiles += [first[h], second[h]]
+                if h < 3:
+                    tiles.append(jnp.where(sub < 6 - 2 * h, extra[h], turned[h + 1]))
+        rows = jnp.concatenate(tiles, axis=0).astype(BF16)
+        out[pl.ds(pl.multiple_of(8 * MSG * k, 8 * MSG), 8 * MSG), :] = rows
         return carry
 
-    lax.fori_loop(0, NSPACE // 2, emit, 0, unroll=4)
-
-
-def collect(got, tag_pick, spread, coef, out):
+    lax.fori_loop(0, NSPACE // 8, emit, 0)
+
+
+def collect(place, got, col, out):
     x = got[...]
-    tags = jnp.dot(tag_pick[...], x, preferred_element_type=F32).astype(BF16)
-    label = jnp.dot(tags, spread[...], preferred_element_type=F32)[0:1]
-    goal = jnp.where(label > 0.5, label * coef[0:1] + coef[1:2], -1.0)
-    row = lax.broadcasted_iota(jnp.int32, (PART, NSPACE * MSG), 0).astype(F32)
+    columns = NSPACE * MSG
+    turn = (2 * (place[0] & 3)).astype(F32)
+    at = col[0:1] - turn
+    at = jnp.where(at < 0, at + MSG, at)
+    src = col[1:2]
+    main = at < 15.5
+    rank = jnp.where(main, jnp.where(at < 7.5, 0.0, 1.0), jnp.where(at < 17.5, 0.0, 1.0))
+    slot = jnp.where(at < 19.5, 2 * src + rank, -1.0)
+    row = lax.broadcasted_iota(jnp.int32, (PART, columns), 0).astype(F32)
+    spread = jnp.where(row[0:SLOTS] == slot, 1.0, 0.0).astype(BF16)
+    tag_row = jnp.where(jnp.abs(at - 20) < 0.5, 0.0, -1.0)
+    tag_pick = jnp.where(row[0:16] == tag_row, 1.0, 0.0).astype(BF16)
+    tags = jnp.dot(tag_pick, x, preferred_element_type=F32).astype(BF16)
+    label = jnp.dot(tags, spread, preferred_element_type=F32)[0:1]
+    goal = jnp.where(main, 8 * label + (24 + at - 8 * rank), 2 * label + (at - 18 - 2 * rank))
+    goal = jnp.where(label > 0.5, goal, -1.0)
     route = jnp.where(row == goal, 1.0, 0.0).astype(BF16)
     part = jnp.dot(route, x, preferred_element_type=F32).astype(BF16)
     for j in range(NCHAN):
@@ -180,27 +203,15 @@
 
 def tables():
     j = np.arange(NSPACE * MSG)
-    src, t, r = j // MSG, (j % MSG) // 8, j % 8
-    rank = np.where(t < 2, t, r // 2)
-    data = (t < 2) | (r < 4)
-    tag_pick = np.zeros((16, j.size), np.float32)
-    tag_pick[0] = (t == 2) & (r == 4)
-    spread = (np.arange(SLOTS)[:, None] == (2 * src + rank)[None]) & data[None]
-    coef = np.zeros((8, j.size), np.float32)
-    coef[0] = np.where(t < 2, 8, 2)
-    coef[1] = np.where(t < 2, 32 - 8 + r, -2 + (r & 1))
+    col = np.zeros((8, j.size), np.float32)
+    col[0] = j % MSG
+    col[1] = j // MSG
     k = np.arange(256)
     c, i = (k % 128) // 16, k % 16
     var = OWN * c + np.where(k < 128, i % 8, 8 + i % 2)
     proj = np.arange(VARS)[:, None] == var[None]
     fold = var[:, None] == np.arange(B)[None]
-    return (
-        tag_pick.astype(BF16),
-        spread.astype(BF16),
-        coef,
-        proj.astype(BF16),
-        fold.astype(np.float32),
-    )
+    return col, proj.astype(BF16), fold.astype(np.float32)
 
 
 def small_grant(mib):
@@ -216,7 +227,7 @@
 
 
 def on_device(cotangent, pair_band, pair_target, pair_count, pair_weight, head_weight, features):
-    tag_pick, spread, coef, proj, fold = tables()
+    col, proj, fold = tables()
     hp_local = features.shape[1]
     place = lax.axis_index(("chan",) + SPACE).astype(jnp.int32).reshape(1)
     hbm = pl.BlockSpec(memory_space=pltpu.HBM)
@@ -237,13 +248,15 @@
         compiler_params=small_grant(12),
         name="contribute",
     )(place, pair_count, *map(far, (pair_band, pair_target, cotangent, pair_weight)))
-    got = lax.all_to_all(sent.reshape(NSPACE, MSG, B), SPACE, 0, 0, tiled=True)
+    got = lax.all_to_all(sent.reshape(NSPACE, MSG // 2, 2, B), SPACE, 0, 0, tiled=True)
     parts = pl.pallas_call(
         collect,
         out_shape=jax.ShapeDtypeStruct((NCHAN, PART, B), BF16),
+        in_specs=[pl.BlockSpec(memory_space=pltpu.SMEM)]
+        + [pl.BlockSpec(memory_space=pltpu.VMEM)] * 2,
         compiler_params=small_grant(8),
         name="collect",
-    )(near(got.reshape(NSPACE * MSG, B)), tag_pick, spread, coef)
+    )(place, near(got.reshape(NSPACE * MSG, B)), col)
     parts = lax.all_to_all(parts, "chan", 0, 0, tiled=True).reshape(NCHAN * PART, B)
     parts = near(parts)
     feature_grad, share = pl.pallas_call(

time: 76.1 us -> 75.6 us (level)
  no operation moved by 1% of the time
where the time goes in v6:
time: 75.6 us; the launch traced here: 75.3 us
  blocking collectives  68.3 us (90%)
  Pallas kernels  5.52 us (7%)
  between operations  1.43 us (2%)
    all_to_all x1, blocking collectives, on_device(): lax.all_to_all(sent.reshape(NSPACE, MSG // 2, 2, B), SPACE, 0, 0, tiled=T...  24.9 us
    all_to_all x1, blocking collectives, on_device(): lax.all_to_all(parts, 'chan', 0, 0, tiled=True).reshape(NCHAN * PART, B)  22.9 us
    all_to_all x1, blocking collectives, on_device(): share = lax.all_to_all(share, 'y', 0, 0, tiled=True)  10.7 us
    all_to_all x1, blocking collectives, on_device(): share = lax.all_to_all(share, ('x', 'core'), 0, 0, tiled=True)  9.85 us
    pallas_call x1, Pallas kernels, on_device(): pl.pallas_call(contribute, out_shape=jax.ShapeDtypeStruct((NSPACE * MSG,...  3.06 us

profile of v6, /device:TPU:1, one launch (start us, length us, event | category | flops | bytes accessed | tf_op | source)
XLA Modules:
  0.0 75.3 jit_solution(1679477215138673136)
XLA Ops:
  0.6 0.0 copy-start.2
  0.6 0.0 copy-start.1
  0.7 0.0 copy-start.3
  0.7 0.0 copy-start
  0.7 0.0 copy-start.4
  1.4 3.1 %contribute.1 = bf16[1408,128]{1,0:T(8,128)(2,1)S(1)} custom-call(s32[1]{0:T(128)} %bitcast.place, s32[1]{0:T(128)S(6)} %copy.12.count, s32[128]{0:T(128)} %band_in.1, s32[128]{0:T(128)} %target_in.1, bf16[80,2048]{1,0:T(8,128)(2,1)} %cot_in.1, bf16[128,128,128]{2,1,0:T(8,128)(2,1)} %weight_in.1), custom_call_target="tpu_custom_call" | custom-call | tf_op jit(solution)/shard_map/contribute/pallas_call | solution.py:234
  4.5 24.9 %all_to_all.20 = bf16[64,11,2,128]{3,2,1,0:T(2,128)(2,1)S(1)} all-to-all(bf16[64,11,2,128]{3,2,1,0:T(2,128)(2,1)S(1)} %bitcast.5), channel_id=1, replica_groups=mesh['chan'=8,'y'=8,'x'=4,'core'=2] {'y','x','core'}, dimensions={0} | all-to-all | bytes 720896 | tf_op jit(solution)/shard_map/all_to_all | solution.py:251
  29.4 0.0 copy-done.2
  29.4 0.6 collect.1
  30.0 22.9 %all_to_all.21 = bf16[8,160,128]{2,1,0:T(8,128)(2,1)S(1)} all-to-all(bf16[8,160,128]{2,1,0:T(8,128)(2,1)S(1)} %collect.1), channel_id=1, replica_groups=mesh['chan'=8,'y'=8,'x'=4,'core'=2] {'chan'}, dimensions={0} | all-to-all | bytes 655360 | tf_op jit(solution)/shard_map/all_to_all | solution.py:260
  52.9 0.0 copy-done.1
  52.9 0.0 copy-done.3
  52.9 0.0 copy-done
  52.9 0.0 copy-done.4
  52.9 1.1 %heads.1 = (bf16[64,2048]{1,0:T(8,128)(2,1)}, f32[8,40,128]{2,1,0:T(8,128)S(1)}) custom-call(bf16[1280,128]{1,0:T(8,128)(2,1)S(1)} %bitcast.6, bf16[64,2048]{1,0:T(8,128)(2,1)S(1)} %copy-done, bf16[64,80]{1,0:T(8,128)(2,1)S(1)} %copy-done.4, bf16[80,256]{1,0:T(8,128)(2,1)S(1)} %copy-done.3, f32[256,128]{1,0:T(8,128)S(1)} %copy-done.1), custom_call_target="tpu_custom_call" | custom-call | tf_op jit(solution)/shard_map/heads/pallas_call | solution.py:262
  54.1 9.8 %all_to_all.22.got = f32[8,40,128]{2,1,0:T(8,128)S(1)} all-to-all(f32[8,40,128]{2,1,0:T(8,128)S(1)} %get-tuple-element.5), channel_id=1, replica_groups=mesh['chan'=8,'y'=8,'x'=4,'core'=2] {'x','core'}, dimensions={0} | all-to-all | bytes 327680 | tf_op jit(solution)/shard_map/all_to_all | solution.py:277
  63.9 10.7 %all_to_all.23.got = f32[8,40,128]{2,1,0:T(8,128)S(1)} all-to-all(f32[8,40,128]{2,1,0:T(8,128)S(1)} %add_copies.1), channel_id=1, replica_groups=mesh['chan'=8,'y'=8,'x'=4,'core'=2] {'y'}, dimensions={0} | all-to-all | bytes 327680 | tf_op jit(solution)/shard_map/all_to_all | solution.py:284
  74.6 0.7 add_last.1
  (1 shorter events, 0.0 us)
Async XLA Ops:
  0.6 28.7 %copy-start.2 = (f32[8,1408]{1,0:T(8,128)S(1)}, f32[8,1408]{1,0:T(8,128)}, u32[]{:S(2)}) copy-start(f32[8,1408]{1,0:T(8,128)} %constant.28.clone.col) | copy-start | bytes 135172
  0.6 52.2 %copy-start.1 = (f32[256,128]{1,0:T(8,128)S(1)}, f32[256,128]{1,0:T(8,128)}, u32[]{:S(2)}) copy-start(f32[256,128]{1,0:T(8,128)} %constant.30.clone.fold) | copy-start | bytes 393220
  0.7 52.2 %copy-start.3 = (bf16[80,256]{1,0:T(8,128)(2,1)S(1)}, bf16[80,256]{1,0:T(8,128)(2,1)}, u32[]{:S(2)}) copy-start(bf16[80,256]{1,0:T(8,128)(2,1)} %constant.29.clone.proj) | copy-start | bytes 122884
  0.7 52.2 %copy-start = (bf16[64,2048]{1,0:T(8,128)(2,1)S(1)}, bf16[64,2048]{1,0:T(8,128)(2,1)}, u32[]{:S(2)}) copy-start(bf16[64,2048]{1,0:T(8,128)(2,1)} %features.1) | copy-start | bytes 786436
  0.7 52.2 %copy-start.4 = (bf16[64,80]{1,0:T(8,128)(2,1)S(1)}, bf16[64,80]{1,0:T(8,128)(2,1)}, u32[]{:S(2)}) copy-start(bf16[64,80]{1,0:T(8,128)(2,1)} %head.1) | copy-start | bytes 30724

commit v7 on v6

--- a/solution.py
+++ b/solution.py
@@ -141,38 +141,63 @@
         out[j] = part
 
 
-def widen(parts, wide):
-    row = lax.broadcasted_iota(jnp.int32, (16, B), 0)
-    main = [jnp.where((row >> 3) == k, 1.0, 0.0).astype(BF16) for k in range(2)]
-    tail = [jnp.where((row >> 1) == k, 1.0, 0.0).astype(BF16) for k in range(8)]
-    for b in range(BLOCKS):
-        for c in range(NCHAN):
-            base = PART * c + 32 + 16 * (b // 2)
-            wide[16 * c : 16 * c + 16, b * B : (b + 1) * B] = parts[base : base + 16] * main[b % 2]
-            base = PART * c + 16 * (b // 8)
-            wide[128 + 16 * c : 144 + 16 * c, b * B : (b + 1) * B] = (
-                parts[base : base + 16] * tail[b % 8]
-            )
-
-
-def heads(parts, features, head, proj, fold, grad_out, share, wide, grad, sem):
-    widen(parts, wide)
-    lifted = jnp.dot(head[...], proj[...], preferred_element_type=F32).astype(BF16)
-    grad[...] = jnp.dot(lifted, wide[...], preferred_element_type=F32).astype(BF16)
+def heads(parts, features, head, proj, fold, grad_out, share, grad, sem):
+    def gather(at):
+        return jnp.concatenate(
+            [parts[PART * c + at : PART * c + at + 16] for c in range(NCHAN)], axis=0
+        )
+
+    tails = [gather(16 * k) for k in range(2)]
+    mains = [gather(32 + 16 * k) for k in range(8)]
+    lane = lax.broadcasted_iota(jnp.int32, (64, B), 1) & 15
+    lifted = jnp.dot(head[...], proj[...], preferred_element_type=F32)
+    low = [jnp.where((lane >> 3) == k, lifted[:, 0:B], 0.0).astype(BF16) for k in range(2)]
+    high = [jnp.where((lane >> 1) == k, lifted[:, B:], 0.0).astype(BF16) for k in range(8)]
+    for pair in range(BLOCKS // 2):
+        left = jnp.concatenate(
+            [
+                jnp.concatenate([low[k], high[(2 * pair + k) % 8]], axis=1)
+                for k in range(2)
+            ],
+            axis=0,
+        )
+        right = jnp.concatenate([mains[pair], tails[pair // 4]], axis=0)
+        both = jnp.dot(left, right, preferred_element_type=F32).astype(BF16)
+        for k in range(2):
+            grad[:, (2 * pair + k) * B : (2 * pair + k + 1) * B] = both[64 * k : 64 * k + 64]
     copy = pltpu.make_async_copy(grad, grad_out, sem)
     copy.start()
-    total = lax.dot_general(
-        features[...], wide[...], (((1,), (1,)), ((), ())), preferred_element_type=F32
+
+    def block(b):
+        return features[:, b * B : (b + 1) * B]
+
+    def product(left, right):
+        return lax.dot_general(left, right, (((1,), (1,)), ((), ())), preferred_element_type=F32)
+
+    paired = [
+        jnp.concatenate([block(2 * k + half) for k in range(8)], axis=1) for half in range(2)
+    ]
+    total_main = product(jnp.concatenate(paired, axis=0), jnp.concatenate(mains, axis=1))
+    eight = [jnp.concatenate([block(k), block(8 + k)], axis=1) for k in range(8)]
+    total_tail = product(jnp.concatenate(eight, axis=0), jnp.concatenate(tails, axis=1))
+    main = jnp.where((lane >> 3) == 0, total_main[0:64], total_main[64:128])
+    tail = total_tail[0:64]
+    for k in range(1, 8):
+        tail = jnp.where((lane >> 1) == k, total_tail[64 * k : 64 * k + 64], tail)
+    total = jnp.dot(
+        jnp.concatenate([main, tail], axis=1),
+        fold[...],
+        preferred_element_type=F32,
+        precision=lax.Precision.HIGHEST,
     )
-    total = jnp.dot(total, fold[...], preferred_element_type=F32, precision=lax.Precision.HIGHEST)
-    lane = lax.broadcasted_iota(jnp.int32, (64, B), 1)
-    low = jnp.where(lane < 64, total, 0.0)
-    high = jnp.where(lane < 64, 0.0, total)
-    front = low[0:32] + pltpu.roll(low[32:64], 64, 1)
-    back = high[32:40]
+    full = lax.broadcasted_iota(jnp.int32, (64, B), 1)
+    first = jnp.where(full < 64, total, 0.0)
+    rest = jnp.where(full < 64, 0.0, total)
+    front = first[0:32] + pltpu.roll(first[32:64], 64, 1)
+    back = rest[32:40]
     for k in range(8):
         if k != 4:
-            back = back + pltpu.roll(high[8 * k : 8 * k + 8], (16 * k - 64) % B, 1)
+            back = back + pltpu.roll(rest[8 * k : 8 * k + 8], (16 * k - 64) % B, 1)
     for j in range(GROUP):
         share[j, 0:32] = front
         share[j, 32:40] = back
@@ -267,7 +292,6 @@
         ),
         out_specs=(hbm, pl.BlockSpec(memory_space=pltpu.VMEM)),
         scratch_shapes=[
-            pltpu.VMEM((256, hp_local), BF16),
             pltpu.VMEM((head_weight.shape[0], hp_local), BF16),
             pltpu.SemaphoreType.DMA(()),
         ],

time: 75.6 us -> 75.6 us (level)
  no operation moved by 1% of the time
where the time goes in v7:
time: 75.6 us; the launch traced here: 75.3 us
  blocking collectives  68.3 us (90%)
  Pallas kernels  5.5 us (7%)
  between operations  1.43 us (2%)
    all_to_all x1, blocking collectives, on_device(): lax.all_to_all(sent.reshape(NSPACE, MSG // 2, 2, B), SPACE, 0, 0, tiled=T...  24.9 us
    all_to_all x1, blocking collectives, on_device(): lax.all_to_all(parts, 'chan', 0, 0, tiled=True).reshape(NCHAN * PART, B)  22.9 us
    all_to_all x1, blocking collectives, on_device(): share = lax.all_to_all(share, 'y', 0, 0, tiled=True)  10.7 us
    all_to_all x1, blocking collectives, on_device(): share = lax.all_to_all(share, ('x', 'core'), 0, 0, tiled=True)  9.85 us
    pallas_call x1, Pallas kernels, on_device(): pl.pallas_call(contribute, out_shape=jax.ShapeDtypeStruct((NSPACE * MSG,...  3.06 us

profile of v7, /device:TPU:1, one launch (start us, length us, event | category | flops | bytes accessed | tf_op | source)
XLA Modules:
  0.0 75.3 jit_solution(4974210812143869635)
XLA Ops:
  0.6 0.0 copy-start.2
  0.6 0.0 copy-start.1
  0.7 0.0 copy-start.3
  0.7 0.0 copy-start
  0.7 0.0 copy-start.4
  1.4 3.1 %contribute.1 = bf16[1408,128]{1,0:T(8,128)(2,1)S(1)} custom-call(s32[1]{0:T(128)} %bitcast.place, s32[1]{0:T(128)S(6)} %copy.12.count, s32[128]{0:T(128)} %band_in.1, s32[128]{0:T(128)} %target_in.1, bf16[80,2048]{1,0:T(8,128)(2,1)} %cot_in.1, bf16[128,128,128]{2,1,0:T(8,128)(2,1)} %weight_in.1), custom_call_target="tpu_custom_call" | custom-call | tf_op jit(solution)/shard_map/contribute/pallas_call | solution.py:259
  4.5 24.9 %all_to_all.20 = bf16[64,11,2,128]{3,2,1,0:T(2,128)(2,1)S(1)} all-to-all(bf16[64,11,2,128]{3,2,1,0:T(2,128)(2,1)S(1)} %bitcast.5), channel_id=1, replica_groups=mesh['chan'=8,'y'=8,'x'=4,'core'=2] {'y','x','core'}, dimensions={0} | all-to-all | bytes 720896 | tf_op jit(solution)/shard_map/all_to_all | solution.py:276
  29.4 0.0 copy-done.2
  29.4 0.6 collect.1
  30.0 22.9 %all_to_all.21 = bf16[8,160,128]{2,1,0:T(8,128)(2,1)S(1)} all-to-all(bf16[8,160,128]{2,1,0:T(8,128)(2,1)S(1)} %collect.1), channel_id=1, replica_groups=mesh['chan'=8,'y'=8,'x'=4,'core'=2] {'chan'}, dimensions={0} | all-to-all | bytes 655360 | tf_op jit(solution)/shard_map/all_to_all | solution.py:285
  52.9 0.0 copy-done.1
  52.9 0.0 copy-done.3
  52.9 0.0 copy-done
  52.9 0.0 copy-done.4
  52.9 1.1 %heads.1 = (bf16[64,2048]{1,0:T(8,128)(2,1)}, f32[8,40,128]{2,1,0:T(8,128)S(1)}) custom-call(bf16[1280,128]{1,0:T(8,128)(2,1)S(1)} %bitcast.6, bf16[64,2048]{1,0:T(8,128)(2,1)S(1)} %copy-done, bf16[64,80]{1,0:T(8,128)(2,1)S(1)} %copy-done.4, bf16[80,256]{1,0:T(8,128)(2,1)S(1)} %copy-done.3, f32[256,128]{1,0:T(8,128)S(1)} %copy-done.1), custom_call_target="tpu_custom_call" | custom-call | tf_op jit(solution)/shard_map/heads/pallas_call | solution.py:287
  54.0 9.8 %all_to_all.22.got = f32[8,40,128]{2,1,0:T(8,128)S(1)} all-to-all(f32[8,40,128]{2,1,0:T(8,128)S(1)} %get-tuple-element.5), channel_id=1, replica_groups=mesh['chan'=8,'y'=8,'x'=4,'core'=2] {'x','core'}, dimensions={0} | all-to-all | bytes 327680 | tf_op jit(solution)/shard_map/all_to_all | solution.py:301
  63.9 10.7 %all_to_all.23.got = f32[8,40,128]{2,1,0:T(8,128)S(1)} all-to-all(f32[8,40,128]{2,1,0:T(8,128)S(1)} %add_copies.1), channel_id=1, replica_groups=mesh['chan'=8,'y'=8,'x'=4,'core'=2] {'y'}, dimensions={0} | all-to-all | bytes 327680 | tf_op jit(solution)/shard_map/all_to_all | solution.py:308
  74.6 0.7 add_last.1
  (1 shorter events, 0.0 us)
Async XLA Ops:
  0.6 28.7 %copy-start.2 = (f32[8,1408]{1,0:T(8,128)S(1)}, f32[8,1408]{1,0:T(8,128)}, u32[]{:S(2)}) copy-start(f32[8,1408]{1,0:T(8,128)} %constant.28.clone.col) | copy-start | bytes 135172
  0.6 52.2 %copy-start.1 = (f32[256,128]{1,0:T(8,128)S(1)}, f32[256,128]{1,0:T(8,128)}, u32[]{:S(2)}) copy-start(f32[256,128]{1,0:T(8,128)} %constant.30.clone.fold) | copy-start | bytes 393220
  0.7 52.2 %copy-start.3 = (bf16[80,256]{1,0:T(8,128)(2,1)S(1)}, bf16[80,256]{1,0:T(8,128)(2,1)}, u32[]{:S(2)}) copy-start(bf16[80,256]{1,0:T(8,128)(2,1)} %constant.29.clone.proj) | copy-start | bytes 122884
  0.7 52.2 %copy-start = (bf16[64,2048]{1,0:T(8,128)(2,1)S(1)}, bf16[64,2048]{1,0:T(8,128)(2,1)}, u32[]{:S(2)}) copy-start(bf16[64,2048]{1,0:T(8,128)(2,1)} %features.1) | copy-start | bytes 786436
  0.7 52.2 %copy-start.4 = (bf16[64,80]{1,0:T(8,128)(2,1)S(1)}, bf16[64,80]{1,0:T(8,128)(2,1)}, u32[]{:S(2)}) copy-start(bf16[64,80]{1,0:T(8,128)(2,1)} %head.1) | copy-start | bytes 30724

commit v8 on v7

--- a/solution.py
+++ b/solution.py
@@ -141,7 +141,7 @@
         out[j] = part
 
 
-def heads(parts, features, head, proj, fold, grad_out, share, grad, sem):
+def heads(parts, features, head, proj, fold, grad, share):
     def gather(at):
         return jnp.concatenate(
             [parts[PART * c + at : PART * c + at + 16] for c in range(NCHAN)], axis=0
@@ -165,8 +165,6 @@
         both = jnp.dot(left, right, preferred_element_type=F32).astype(BF16)
         for k in range(2):
             grad[:, (2 * pair + k) * B : (2 * pair + k + 1) * B] = both[64 * k : 64 * k + 64]
-    copy = pltpu.make_async_copy(grad, grad_out, sem)
-    copy.start()
 
     def block(b):
         return features[:, b * B : (b + 1) * B]
@@ -201,7 +199,6 @@
     for j in range(GROUP):
         share[j, 0:32] = front
         share[j, 32:40] = back
-    copy.wait()
 
 
 def add_up(got):
@@ -217,13 +214,16 @@
         out[j] = total
 
 
-def add_last(scale, got, out):
+def add_last(scale, got, grad, out, grad_out, sem):
+    copy = pltpu.make_async_copy(grad, grad_out, sem)
+    copy.start()
     total = add_up(got) * scale
     front, back = total[0:32], total[32:40]
     out[0:32, 0:64] = front[:, 0:64]
     out[32:64, 0:64] = pltpu.roll(front, 64, 1)[:, 0:64]
     for k in range(8):
         out[8 * k : 8 * k + 8, 64:VARS] = pltpu.roll(back, (64 - 16 * k) % B, 1)[:, 64:VARS]
+    copy.wait()
 
 
 def tables():
@@ -290,11 +290,7 @@
             jax.ShapeDtypeStruct((head_weight.shape[0], hp_local), BF16),
             jax.ShapeDtypeStruct((GROUP, 40, B), F32),
         ),
-        out_specs=(hbm, pl.BlockSpec(memory_space=pltpu.VMEM)),
-        scratch_shapes=[
-            pltpu.VMEM((head_weight.shape[0], hp_local), BF16),
-            pltpu.SemaphoreType.DMA(()),
-        ],
+        out_specs=(pl.BlockSpec(memory_space=pltpu.VMEM),) * 2,
         compiler_params=small_grant(8),
         name="heads",
     )(parts, features, head_weight, proj, fold)
@@ -307,12 +303,17 @@
     )(near(share))
     share = lax.all_to_all(share, "y", 0, 0, tiled=True)
     grad_scale = float(hp_local * NSPACE) ** (-0.5)
-    weight_grad = pl.pallas_call(
+    weight_grad, feature_grad = pl.pallas_call(
         functools.partial(add_last, grad_scale),
-        out_shape=jax.ShapeDtypeStruct(head_weight.shape, F32),
+        out_shape=(
+            jax.ShapeDtypeStruct(head_weight.shape, F32),
+            jax.ShapeDtypeStruct(feature_grad.shape, BF16),
+        ),
+        out_specs=(pl.BlockSpec(memory_space=pltpu.VMEM), hbm),
+        scratch_shapes=[pltpu.SemaphoreType.DMA(())],
         compiler_params=small_grant(2),
         name="add_last",
-    )(near(share))
+    )(near(share), near(feature_grad))
     return feature_grad, weight_grad
 
 

time: 75.6 us -> 75.9 us (level)
  no operation moved by 1% of the time
where the time goes in v8:
time: 75.9 us; the launch traced here: 75.6 us
  blocking collectives  68.3 us (90%)
  Pallas kernels  5.8 us (8%)
  between operations  1.43 us (2%)
    all_to_all x1, blocking collectives, on_device(): lax.all_to_all(sent.reshape(NSPACE, MSG // 2, 2, B), SPACE, 0, 0, tiled=T...  24.9 us
    all_to_all x1, blocking collectives, on_device(): lax.all_to_all(parts, 'chan', 0, 0, tiled=True).reshape(NCHAN * PART, B)  22.9 us
    all_to_all x1, blocking collectives, on_device(): share = lax.all_to_all(share, 'y', 0, 0, tiled=True)  10.7 us
    all_to_all x1, blocking collectives, on_device(): share = lax.all_to_all(share, ('x', 'core'), 0, 0, tiled=True)  9.85 us
    pallas_call x1, Pallas kernels, on_device(): pl.pallas_call(contribute, out_shape=jax.ShapeDtypeStruct((NSPACE * MSG,...  3.06 us

profile of v8, /device:TPU:1, one launch (start us, length us, event | category | flops | bytes accessed | tf_op | source)
XLA Modules:
  0.0 75.6 jit_solution(826755800734782619)
XLA Ops:
  0.6 0.0 copy-start.2
  0.6 0.0 copy-start.1
  0.7 0.0 copy-start.3
  0.7 0.0 copy-start
  0.7 0.0 copy-start.4
  1.4 3.1 %contribute.1 = bf16[1408,128]{1,0:T(8,128)(2,1)S(1)} custom-call(s32[1]{0:T(128)} %bitcast.place, s32[1]{0:T(128)S(6)} %copy.12.count, s32[128]{0:T(128)} %band_in.1, s32[128]{0:T(128)} %target_in.1, bf16[80,2048]{1,0:T(8,128)(2,1)} %cot_in.1, bf16[128,128,128]{2,1,0:T(8,128)(2,1)} %weight_in.1), custom_call_target="tpu_custom_call" | custom-call | tf_op jit(solution)/shard_map/contribute/pallas_call | solution.py:259
  4.5 24.9 %all_to_all.20 = bf16[64,11,2,128]{3,2,1,0:T(2,128)(2,1)S(1)} all-to-all(bf16[64,11,2,128]{3,2,1,0:T(2,128)(2,1)S(1)} %bitcast.5), channel_id=1, replica_groups=mesh['chan'=8,'y'=8,'x'=4,'core'=2] {'y','x','core'}, dimensions={0} | all-to-all | bytes 720896 | tf_op jit(solution)/shard_map/all_to_all | solution.py:276
  29.4 0.0 copy-done.2
  29.4 0.6 collect.1
  30.0 22.9 %all_to_all.21 = bf16[8,160,128]{2,1,0:T(8,128)(2,1)S(1)} all-to-all(bf16[8,160,128]{2,1,0:T(8,128)(2,1)S(1)} %collect.1), channel_id=1, replica_groups=mesh['chan'=8,'y'=8,'x'=4,'core'=2] {'chan'}, dimensions={0} | all-to-all | bytes 655360 | tf_op jit(solution)/shard_map/all_to_all | solution.py:285
  52.9 0.0 copy-done.1
  52.9 0.0 copy-done.3
  52.9 0.0 copy-done
  52.9 0.0 copy-done.4
  52.9 0.8 %heads.1 = (bf16[64,2048]{1,0:T(8,128)(2,1)S(1)}, f32[8,40,128]{2,1,0:T(8,128)S(1)}) custom-call(bf16[1280,128]{1,0:T(8,128)(2,1)S(1)} %bitcast.6, bf16[64,2048]{1,0:T(8,128)(2,1)S(1)} %copy-done, bf16[64,80]{1,0:T(8,128)(2,1)S(1)} %copy-done.4, bf16[80,256]{1,0:T(8,128)(2,1)S(1)} %copy-done.3, f32[256,128]{1,0:T(8,128)S(1)} %copy-done.1), custom_call_target="tpu_custom_call" | custom-call | tf_op jit(solution)/shard_map/heads/pallas_call | solution.py:287
  53.7 9.8 %all_to_all.22.got = f32[8,40,128]{2,1,0:T(8,128)S(1)} all-to-all(f32[8,40,128]{2,1,0:T(8,128)S(1)} %get-tuple-element.6), channel_id=1, replica_groups=mesh['chan'=8,'y'=8,'x'=4,'core'=2] {'x','core'}, dimensions={0} | all-to-all | bytes 327680 | tf_op jit(solution)/shard_map/all_to_all | solution.py:297
  63.6 10.7 %all_to_all.23.got = f32[8,40,128]{2,1,0:T(8,128)S(1)} all-to-all(f32[8,40,128]{2,1,0:T(8,128)S(1)} %add_copies.1), channel_id=1, replica_groups=mesh['chan'=8,'y'=8,'x'=4,'core'=2] {'y'}, dimensions={0} | all-to-all | bytes 327680 | tf_op jit(solution)/shard_map/all_to_all | solution.py:304
  74.2 1.3 %add_last.1 = (f32[64,80]{1,0:T(8,128)}, bf16[64,2048]{1,0:T(8,128)(2,1)}) custom-call(f32[8,40,128]{2,1,0:T(8,128)S(1)} %all_to_all.23.got, bf16[64,2048]{1,0:T(8,128)(2,1)S(1)} %get-tuple-element.7.grad), custom_call_target="tpu_custom_call" | custom-call | tf_op jit(solution)/shard_map/add_last/pallas_call | solution.py:306
  (1 shorter events, 0.0 us)
Async XLA Ops:
  0.6 28.7 %copy-start.2 = (f32[8,1408]{1,0:T(8,128)S(1)}, f32[8,1408]{1,0:T(8,128)}, u32[]{:S(2)}) copy-start(f32[8,1408]{1,0:T(8,128)} %constant.28.clone.col) | copy-start | bytes 135172
  0.6 52.2 %copy-start.1 = (f32[256,128]{1,0:T(8,128)S(1)}, f32[256,128]{1,0:T(8,128)}, u32[]{:S(2)}) copy-start(f32[256,128]{1,0:T(8,128)} %constant.30.clone.fold) | copy-start | bytes 393220
  0.7 52.2 %copy-start.3 = (bf16[80,256]{1,0:T(8,128)(2,1)S(1)}, bf16[80,256]{1,0:T(8,128)(2,1)}, u32[]{:S(2)}) copy-start(bf16[80,256]{1,0:T(8,128)(2,1)} %constant.29.clone.proj) | copy-start | bytes 122884
  0.7 52.2 %copy-start = (bf16[64,2048]{1,0:T(8,128)(2,1)S(1)}, bf16[64,2048]{1,0:T(8,128)(2,1)}, u32[]{:S(2)}) copy-start(bf16[64,2048]{1,0:T(8,128)(2,1)} %features.1) | copy-start | bytes 786436
  0.7 52.2 %copy-start.4 = (bf16[64,80]{1,0:T(8,128)(2,1)S(1)}, bf16[64,80]{1,0:T(8,128)(2,1)}, u32[]{:S(2)}) copy-start(bf16[64,80]{1,0:T(8,128)(2,1)} %head.1) | copy-start | bytes 30724

commit v9 on v7

--- a/solution.py
+++ b/solution.py
@@ -153,6 +153,7 @@
     lifted = jnp.dot(head[...], proj[...], preferred_element_type=F32)
     low = [jnp.where((lane >> 3) == k, lifted[:, 0:B], 0.0).astype(BF16) for k in range(2)]
     high = [jnp.where((lane >> 1) == k, lifted[:, B:], 0.0).astype(BF16) for k in range(8)]
+    copies = []
     for pair in range(BLOCKS // 2):
         left = jnp.concatenate(
             [
@@ -165,8 +166,12 @@
         both = jnp.dot(left, right, preferred_element_type=F32).astype(BF16)
         for k in range(2):
             grad[:, (2 * pair + k) * B : (2 * pair + k + 1) * B] = both[64 * k : 64 * k + 64]
-    copy = pltpu.make_async_copy(grad, grad_out, sem)
-    copy.start()
+        if pair % 2:
+            at = pl.ds((2 * pair - 2) * B, 4 * B)
+            copies.append(
+                pltpu.make_async_copy(grad.at[:, at], grad_out.at[:, at], sem.at[pair // 2])
+            )
+            copies[-1].start()
 
     def block(b):
         return features[:, b * B : (b + 1) * B]
@@ -201,7 +206,8 @@
     for j in range(GROUP):
         share[j, 0:32] = front
         share[j, 32:40] = back
-    copy.wait()
+    for copy in copies:
+        copy.wait()
 
 
 def add_up(got):
@@ -293,19 +299,19 @@
         out_specs=(hbm, pl.BlockSpec(memory_space=pltpu.VMEM)),
         scratch_shapes=[
             pltpu.VMEM((head_weight.shape[0], hp_local), BF16),
-            pltpu.SemaphoreType.DMA(()),
+            pltpu.SemaphoreType.DMA((4,)),
         ],
         compiler_params=small_grant(8),
         name="heads",
     )(parts, features, head_weight, proj, fold)
-    share = lax.all_to_all(share, ("x", "core"), 0, 0, tiled=True)
+    share = lax.all_to_all(share, "y", 0, 0, tiled=True)
     share = pl.pallas_call(
         add_copies,
         out_shape=jax.ShapeDtypeStruct(share.shape, F32),
         compiler_params=small_grant(2),
         name="add_copies",
     )(near(share))
-    share = lax.all_to_all(share, "y", 0, 0, tiled=True)
+    share = lax.all_to_all(share, ("x", "core"), 0, 0, tiled=True)
     grad_scale = float(hp_local * NSPACE) ** (-0.5)
     weight_grad = pl.pallas_call(
         functools.partial(add_last, grad_scale),

time: 75.6 us -> 76.6 us (1.013)
  blocking collectives: 68.3 us -> 69.5 us
    all_to_all x1, blocking collectives: 9.85 us -> 10.6 us  [on_device(): share = lax.all_to_all(share, ('x', 'core'), 0, 0, tiled=True)]
where the time goes in v9:
time: 76.6 us; the launch traced here: 76.4 us
  blocking collectives  69.5 us (91%)
  Pallas kernels  5.44 us (7%)
  between operations  1.43 us (2%)
    all_to_all x1, blocking collectives, on_device(): lax.all_to_all(sent.reshape(NSPACE, MSG // 2, 2, B), SPACE, 0, 0, tiled=T...  24.9 us
    all_to_all x1, blocking collectives, on_device(): lax.all_to_all(parts, 'chan', 0, 0, tiled=True).reshape(NCHAN * PART, B)  22.9 us
    all_to_all x1, blocking collectives, on_device(): share = lax.all_to_all(share, 'y', 0, 0, tiled=True)  11 us
    all_to_all x1, blocking collectives, on_device(): share = lax.all_to_all(share, ('x', 'core'), 0, 0, tiled=True)  10.6 us
    pallas_call x1, Pallas kernels, on_device(): pl.pallas_call(contribute, out_shape=jax.ShapeDtypeStruct((NSPACE * MSG,...  3.05 us

profile of v9, /device:TPU:1, one launch (start us, length us, event | category | flops | bytes accessed | tf_op | source)
XLA Modules:
  0.0 76.4 jit_solution(9718806626648450430)
XLA Ops:
  0.6 0.0 copy-start.2
  0.6 0.0 copy-start.1
  0.7 0.0 copy-start.3
  0.7 0.0 copy-start
  0.7 0.0 copy-start.4
  1.4 3.1 %contribute.1 = bf16[1408,128]{1,0:T(8,128)(2,1)S(1)} custom-call(s32[1]{0:T(128)} %bitcast.place, s32[1]{0:T(128)S(6)} %copy.12.count, s32[128]{0:T(128)} %band_in.1, s32[128]{0:T(128)} %target_in.1, bf16[80,2048]{1,0:T(8,128)(2,1)} %cot_in.1, bf16[128,128,128]{2,1,0:T(8,128)(2,1)} %weight_in.1), custom_call_target="tpu_custom_call" | custom-call | tf_op jit(solution)/shard_map/contribute/pallas_call | solution.py:265
  4.5 24.9 %all_to_all.20 = bf16[64,11,2,128]{3,2,1,0:T(2,128)(2,1)S(1)} all-to-all(bf16[64,11,2,128]{3,2,1,0:T(2,128)(2,1)S(1)} %bitcast.5), channel_id=1, replica_groups=mesh['chan'=8,'y'=8,'x'=4,'core'=2] {'y','x','core'}, dimensions={0} | all-to-all | bytes 720896 | tf_op jit(solution)/shard_map/all_to_all | solution.py:282
  29.4 0.0 copy-done.2
  29.4 0.6 collect.1
  30.0 22.9 %all_to_all.21 = bf16[8,160,128]{2,1,0:T(8,128)(2,1)S(1)} all-to-all(bf16[8,160,128]{2,1,0:T(8,128)(2,1)S(1)} %collect.1), channel_id=1, replica_groups=mesh['chan'=8,'y'=8,'x'=4,'core'=2] {'chan'}, dimensions={0} | all-to-all | bytes 655360 | tf_op jit(solution)/shard_map/all_to_all | solution.py:291
  52.9 0.0 copy-done.1
  52.9 0.0 copy-done.3
  52.9 0.0 copy-done
  52.9 0.0 copy-done.4
  52.9 1.1 %heads.1 = (bf16[64,2048]{1,0:T(8,128)(2,1)}, f32[8,40,128]{2,1,0:T(8,128)S(1)}) custom-call(bf16[1280,128]{1,0:T(8,128)(2,1)S(1)} %bitcast.6, bf16[64,2048]{1,0:T(8,128)(2,1)S(1)} %copy-done, bf16[64,80]{1,0:T(8,128)(2,1)S(1)} %copy-done.4, bf16[80,256]{1,0:T(8,128)(2,1)S(1)} %copy-done.3, f32[256,128]{1,0:T(8,128)S(1)} %copy-done.1), custom_call_target="tpu_custom_call" | custom-call | tf_op jit(solution)/shard_map/heads/pallas_call | solution.py:293
  54.0 11.0 %all_to_all.22.got = f32[8,40,128]{2,1,0:T(8,128)S(1)} all-to-all(f32[8,40,128]{2,1,0:T(8,128)S(1)} %get-tuple-element.5), channel_id=1, replica_groups=mesh['chan'=8,'y'=8,'x'=4,'core'=2] {'y'}, dimensions={0} | all-to-all | bytes 327680 | tf_op jit(solution)/shard_map/all_to_all | solution.py:307
  65.0 10.6 %all_to_all.23.got = f32[8,40,128]{2,1,0:T(8,128)S(1)} all-to-all(f32[8,40,128]{2,1,0:T(8,128)S(1)} %add_copies.1), channel_id=1, replica_groups=mesh['chan'=8,'y'=8,'x'=4,'core'=2] {'x','core'}, dimensions={0} | all-to-all | bytes 327680 | tf_op jit(solution)/shard_map/all_to_all | solution.py:314
  75.7 0.7 add_last.1
  (1 shorter events, 0.0 us)
Async XLA Ops:
  0.6 28.7 %copy-start.2 = (f32[8,1408]{1,0:T(8,128)S(1)}, f32[8,1408]{1,0:T(8,128)}, u32[]{:S(2)}) copy-start(f32[8,1408]{1,0:T(8,128)} %constant.28.clone.col) | copy-start | bytes 135172
  0.6 52.2 %copy-start.1 = (f32[256,128]{1,0:T(8,128)S(1)}, f32[256,128]{1,0:T(8,128)}, u32[]{:S(2)}) copy-start(f32[256,128]{1,0:T(8,128)} %constant.30.clone.fold) | copy-start | bytes 393220
  0.7 52.2 %copy-start.3 = (bf16[80,256]{1,0:T(8,128)(2,1)S(1)}, bf16[80,256]{1,0:T(8,128)(2,1)}, u32[]{:S(2)}) copy-start(bf16[80,256]{1,0:T(8,128)(2,1)} %constant.29.clone.proj) | copy-start | bytes 122884
  0.7 52.2 %copy-start = (bf16[64,2048]{1,0:T(8,128)(2,1)S(1)}, bf16[64,2048]{1,0:T(8,128)(2,1)}, u32[]{:S(2)}) copy-start(bf16[64,2048]{1,0:T(8,128)(2,1)} %features.1) | copy-start | bytes 786436
  0.7 52.2 %copy-start.4 = (bf16[64,80]{1,0:T(8,128)(2,1)S(1)}, bf16[64,80]{1,0:T(8,128)(2,1)}, u32[]{:S(2)}) copy-start(bf16[64,80]{1,0:T(8,128)(2,1)} %head.1) | copy-start | bytes 30724

commit v10 on v8

--- a/solution.py
+++ b/solution.py
@@ -17,7 +17,7 @@
 BLOCKS = 16
 OWN = VARS // NCHAN
 MSG = 22
-CHUNK = 32
+CHUNK = 16
 PART = OWN * BLOCKS
 GROUP = 8
 SPACE = ("y", "x", "core")
@@ -215,15 +215,20 @@
 
 
 def add_last(scale, got, grad, out, grad_out, sem):
-    copy = pltpu.make_async_copy(grad, grad_out, sem)
-    copy.start()
+    copies = [
+        pltpu.make_async_copy(grad.at[8 * k : 8 * k + 8], grad_out.at[8 * k : 8 * k + 8], sem.at[k])
+        for k in range(8)
+    ]
+    for copy in copies:
+        copy.start()
     total = add_up(got) * scale
     front, back = total[0:32], total[32:40]
     out[0:32, 0:64] = front[:, 0:64]
     out[32:64, 0:64] = pltpu.roll(front, 64, 1)[:, 0:64]
     for k in range(8):
         out[8 * k : 8 * k + 8, 64:VARS] = pltpu.roll(back, (64 - 16 * k) % B, 1)[:, 64:VARS]
-    copy.wait()
+    for copy in copies:
+        copy.wait()
 
 
 def tables():
@@ -310,7 +315,7 @@
             jax.ShapeDtypeStruct(feature_grad.shape, BF16),
         ),
         out_specs=(pl.BlockSpec(memory_space=pltpu.VMEM), hbm),
-        scratch_shapes=[pltpu.SemaphoreType.DMA(())],
+        scratch_shapes=[pltpu.SemaphoreType.DMA((8,))],
         compiler_params=small_grant(2),
         name="add_last",
     )(near(share), near(feature_grad))

time: 75.9 us -> 75.9 us (level)
  no operation moved by 1% of the time
where the time goes in v10:
time: 75.9 us; the launch traced here: 75.6 us
  blocking collectives  68 us (90%)
  Pallas kernels  6.19 us (8%)
  between operations  1.43 us (2%)
    all_to_all x1, blocking collectives, on_device(): lax.all_to_all(sent.reshape(NSPACE, MSG // 2, 2, B), SPACE, 0, 0, tiled=T...  24.9 us
    all_to_all x1, blocking collectives, on_device(): lax.all_to_all(parts, 'chan', 0, 0, tiled=True).reshape(NCHAN * PART, B)  22.6 us
    all_to_all x1, blocking collectives, on_device(): share = lax.all_to_all(share, 'y', 0, 0, tiled=True)  10.7 us
    all_to_all x1, blocking collectives, on_device(): share = lax.all_to_all(share, ('x', 'core'), 0, 0, tiled=True)  9.85 us
    pallas_call x1, Pallas kernels, on_device(): pl.pallas_call(contribute, out_shape=jax.ShapeDtypeStruct((NSPACE * MSG,...  3.4 us

profile of v10, /device:TPU:1, one launch (start us, length us, event | category | flops | bytes accessed | tf_op | source)
XLA Modules:
  0.0 75.6 jit_solution(17051946640728082526)
XLA Ops:
  0.6 0.0 copy-start.2
  0.6 0.0 copy-start.1
  0.7 0.0 copy-start.3
  0.7 0.0 copy-start
  0.7 0.0 copy-start.4
  1.4 3.4 %contribute.1 = bf16[1408,128]{1,0:T(8,128)(2,1)S(1)} custom-call(s32[1]{0:T(128)} %bitcast.place, s32[1]{0:T(128)S(6)} %copy.12.count, s32[128]{0:T(128)} %band_in.1, s32[128]{0:T(128)} %target_in.1, bf16[80,2048]{1,0:T(8,128)(2,1)} %cot_in.1, bf16[128,128,128]{2,1,0:T(8,128)(2,1)} %weight_in.1), custom_call_target="tpu_custom_call" | custom-call | tf_op jit(solution)/shard_map/contribute/pallas_call | solution.py:264
  4.8 24.9 %all_to_all.20 = bf16[64,11,2,128]{3,2,1,0:T(2,128)(2,1)S(1)} all-to-all(bf16[64,11,2,128]{3,2,1,0:T(2,128)(2,1)S(1)} %bitcast.5), channel_id=1, replica_groups=mesh['chan'=8,'y'=8,'x'=4,'core'=2] {'y','x','core'}, dimensions={0} | all-to-all | bytes 720896 | tf_op jit(solution)/shard_map/all_to_all | solution.py:281
  29.7 0.0 copy-done.2
  29.7 0.6 collect.1
  30.3 22.6 %all_to_all.21 = bf16[8,160,128]{2,1,0:T(8,128)(2,1)S(1)} all-to-all(bf16[8,160,128]{2,1,0:T(8,128)(2,1)S(1)} %collect.1), channel_id=1, replica_groups=mesh['chan'=8,'y'=8,'x'=4,'core'=2] {'chan'}, dimensions={0} | all-to-all | bytes 655360 | tf_op jit(solution)/shard_map/all_to_all | solution.py:290
  52.9 0.0 copy-done.1
  52.9 0.0 copy-done.3
  52.9 0.0 copy-done
  52.9 0.0 copy-done.4
  52.9 0.8 %heads.1 = (bf16[64,2048]{1,0:T(8,128)(2,1)S(1)}, f32[8,40,128]{2,1,0:T(8,128)S(1)}) custom-call(bf16[1280,128]{1,0:T(8,128)(2,1)S(1)} %bitcast.6, bf16[64,2048]{1,0:T(8,128)(2,1)S(1)} %copy-done, bf16[64,80]{1,0:T(8,128)(2,1)S(1)} %copy-done.4, bf16[80,256]{1,0:T(8,128)(2,1)S(1)} %copy-done.3, f32[256,128]{1,0:T(8,128)S(1)} %copy-done.1), custom_call_target="tpu_custom_call" | custom-call | tf_op jit(solution)/shard_map/heads/pallas_call | solution.py:292
  53.7 9.8 %all_to_all.22.got = f32[8,40,128]{2,1,0:T(8,128)S(1)} all-to-all(f32[8,40,128]{2,1,0:T(8,128)S(1)} %get-tuple-element.6), channel_id=1, replica_groups=mesh['chan'=8,'y'=8,'x'=4,'core'=2] {'x','core'}, dimensions={0} | all-to-all | bytes 327680 | tf_op jit(solution)/shard_map/all_to_all | solution.py:302
  63.6 10.7 %all_to_all.23.got = f32[8,40,128]{2,1,0:T(8,128)S(1)} all-to-all(f32[8,40,128]{2,1,0:T(8,128)S(1)} %add_copies.1), channel_id=1, replica_groups=mesh['chan'=8,'y'=8,'x'=4,'core'=2] {'y'}, dimensions={0} | all-to-all | bytes 327680 | tf_op jit(solution)/shard_map/all_to_all | solution.py:309
  74.2 1.4 %add_last.1 = (f32[64,80]{1,0:T(8,128)}, bf16[64,2048]{1,0:T(8,128)(2,1)}) custom-call(f32[8,40,128]{2,1,0:T(8,128)S(1)} %all_to_all.23.got, bf16[64,2048]{1,0:T(8,128)(2,1)S(1)} %get-tuple-element.7.grad), custom_call_target="tpu_custom_call" | custom-call | tf_op jit(solution)/shard_map/add_last/pallas_call | solution.py:311
  (1 shorter events, 0.0 us)
Async XLA Ops:
  0.6 29.1 %copy-start.2 = (f32[8,1408]{1,0:T(8,128)S(1)}, f32[8,1408]{1,0:T(8,128)}, u32[]{:S(2)}) copy-start(f32[8,1408]{1,0:T(8,128)} %constant.28.clone.col) | copy-start | bytes 135172
  0.6 52.2 %copy-start.1 = (f32[256,128]{1,0:T(8,128)S(1)}, f32[256,128]{1,0:T(8,128)}, u32[]{:S(2)}) copy-start(f32[256,128]{1,0:T(8,128)} %constant.30.clone.fold) | copy-start | bytes 393220
  0.7 52.2 %copy-start.3 = (bf16[80,256]{1,0:T(8,128)(2,1)S(1)}, bf16[80,256]{1,0:T(8,128)(2,1)}, u32[]{:S(2)}) copy-start(bf16[80,256]{1,0:T(8,128)(2,1)} %constant.29.clone.proj) | copy-start | bytes 122884
  0.7 52.2 %copy-start = (bf16[64,2048]{1,0:T(8,128)(2,1)S(1)}, bf16[64,2048]{1,0:T(8,128)(2,1)}, u32[]{:S(2)}) copy-start(bf16[64,2048]{1,0:T(8,128)(2,1)} %features.1) | copy-start | bytes 786436
  0.7 52.2 %copy-start.4 = (bf16[64,80]{1,0:T(8,128)(2,1)S(1)}, bf16[64,80]{1,0:T(8,128)(2,1)}, u32[]{:S(2)}) copy-start(bf16[64,80]{1,0:T(8,128)(2,1)} %head.1) | copy-start | bytes 30724

commit v11 on v7

--- a/solution.py
+++ b/solution.py
@@ -26,14 +26,14 @@
 
 
 def contribute(
-    place, count, band_in, target_in, cot_in, weight_in, out,
-    band, target, cot, weight, lhs, acc, seen, sems,
+    place, count, band_in, target_in, cot_in, head_in, weight_in, out, tag_pick, spread, left,
+    band, target, cot, head, weight, lhs, acc, seen, sems,
 ):
     chunks = SLOTS // CHUNK
     small = [
         pltpu.make_async_copy(src, dst, sems.at[chunks + k])
         for k, (src, dst) in enumerate(
-            ((cot_in, cot), (band_in, band), (target_in, target))
+            ((cot_in, cot), (band_in, band), (target_in, target), (head_in, head))
         )
     ]
 
@@ -67,12 +67,20 @@
     dead = 2 * BLOCKS
     lhs[dead] = jnp.zeros((16, B), BF16)
     acc[...] = jnp.zeros_like(acc)
+    at, src, _, rank = message_columns(place)
+    lane = lax.broadcasted_iota(jnp.int32, (SLOTS, NSPACE * MSG), 0).astype(F32)
+    slot_of = jnp.where(at < 19.5, 2 * src + rank, -1.0)
+    spread[...] = jnp.where(lane == slot_of, 1.0, 0.0).astype(BF16)
+    tag_row_of = jnp.where(jnp.abs(at - 20) < 0.5, 0.0, -1.0)
+    tag_pick[...] = jnp.where(lane[0:16] == tag_row_of, 1.0, 0.0).astype(BF16)
+    small[3].wait()
+    left_operands(head, left)
     small[0].wait()
     rows = jnp.dot(pick, cot[...], preferred_element_type=F32).astype(BF16)
     for j in range(BLOCKS):
         for rank in range(2):
             lhs[2 * j + rank] = rows[16 * rank : 16 * rank + 16, j * B : (j + 1) * B]
-    for copy in small[1:]:
+    for copy in small[1:3]:
         copy.wait()
 
     def chunk(k, carry):
@@ -117,22 +125,36 @@
     lax.fori_loop(0, NSPACE // 8, emit, 0)
 
 
-def collect(place, got, col, out):
-    x = got[...]
-    columns = NSPACE * MSG
-    turn = (2 * (place[0] & 3)).astype(F32)
-    at = col[0:1] - turn
+def message_columns(place):
+    j = lax.broadcasted_iota(jnp.int32, (1, NSPACE * MSG), 1).astype(F32)
+    src = jnp.floor((j + 0.5) * (1.0 / MSG))
+    at = j - MSG * src - (2 * (place[0] & 3)).astype(F32)
     at = jnp.where(at < 0, at + MSG, at)
-    src = col[1:2]
     main = at < 15.5
     rank = jnp.where(main, jnp.where(at < 7.5, 0.0, 1.0), jnp.where(at < 17.5, 0.0, 1.0))
-    slot = jnp.where(at < 19.5, 2 * src + rank, -1.0)
-    row = lax.broadcasted_iota(jnp.int32, (PART, columns), 0).astype(F32)
-    spread = jnp.where(row[0:SLOTS] == slot, 1.0, 0.0).astype(BF16)
-    tag_row = jnp.where(jnp.abs(at - 20) < 0.5, 0.0, -1.0)
-    tag_pick = jnp.where(row[0:16] == tag_row, 1.0, 0.0).astype(BF16)
-    tags = jnp.dot(tag_pick, x, preferred_element_type=F32).astype(BF16)
-    label = jnp.dot(tags, spread, preferred_element_type=F32)[0:1]
+    return at, src, main, rank
+
+
+def left_operands(head, left):
+    var = lax.broadcasted_iota(jnp.int32, (VARS, 2 * B), 0)
+    col = lax.broadcasted_iota(jnp.int32, (VARS, 2 * B), 1)
+    own = jnp.where(col < B, col & 7, 8 + (col & 1))
+    proj = jnp.where(var == OWN * ((col & (B - 1)) >> 4) + own, 1.0, 0.0).astype(BF16)
+    lifted = jnp.dot(head[...], proj, preferred_element_type=F32)
+    lane = lax.broadcasted_iota(jnp.int32, (64, B), 1) & 15
+    for k in range(8):
+        main = jnp.where((lane >> 3) == k % 2, lifted[:, 0:B], 0.0)
+        tail = jnp.where((lane >> 1) == k, lifted[:, B:], 0.0)
+        left[64 * k : 64 * k + 64, 0:B] = main.astype(BF16)
+        left[64 * k : 64 * k + 64, B : 2 * B] = tail.astype(BF16)
+
+
+def collect(place, got, tag_pick, spread, out):
+    x = got[...]
+    at, _, main, rank = message_columns(place)
+    row = lax.broadcasted_iota(jnp.int32, (PART, NSPACE * MSG), 0).astype(F32)
+    tags = jnp.dot(tag_pick[...], x, preferred_element_type=F32).astype(BF16)
+    label = jnp.dot(tags, spread[...], preferred_element_type=F32)[0:1]
     goal = jnp.where(main, 8 * label + (24 + at - 8 * rank), 2 * label + (at - 18 - 2 * rank))
     goal = jnp.where(label > 0.5, goal, -1.0)
     route = jnp.where(row == goal, 1.0, 0.0).astype(BF16)
@@ -141,7 +163,7 @@
         out[j] = part
 
 
-def heads(parts, features, head, proj, fold, grad_out, share, grad, sem):
+def heads(parts, features, left, fold, grad_out, share, grad, sem):
     def gather(at):
         return jnp.concatenate(
             [parts[PART * c + at : PART * c + at + 16] for c in range(NCHAN)], axis=0
@@ -150,19 +172,10 @@
     tails = [gather(16 * k) for k in range(2)]
     mains = [gather(32 + 16 * k) for k in range(8)]
     lane = lax.broadcasted_iota(jnp.int32, (64, B), 1) & 15
-    lifted = jnp.dot(head[...], proj[...], preferred_element_type=F32)
-    low = [jnp.where((lane >> 3) == k, lifted[:, 0:B], 0.0).astype(BF16) for k in range(2)]
-    high = [jnp.where((lane >> 1) == k, lifted[:, B:], 0.0).astype(BF16) for k in range(8)]
     for pair in range(BLOCKS // 2):
-        left = jnp.concatenate(
-            [
-                jnp.concatenate([low[k], high[(2 * pair + k) % 8]], axis=1)
-                for k in range(2)
-            ],
-            axis=0,
-        )
+        two = 128 * (pair % 4)
         right = jnp.concatenate([mains[pair], tails[pair // 4]], axis=0)
-        both = jnp.dot(left, right, preferred_element_type=F32).astype(BF16)
+        both = jnp.dot(left[two : two + 128], right, preferred_element_type=F32).astype(BF16)
         for k in range(2):
             grad[:, (2 * pair + k) * B : (2 * pair + k + 1) * B] = both[64 * k : 64 * k + 64]
     copy = pltpu.make_async_copy(grad, grad_out, sem)
@@ -227,16 +240,11 @@
 
 
 def tables():
-    j = np.arange(NSPACE * MSG)
-    col = np.zeros((8, j.size), np.float32)
-    col[0] = j % MSG
-    col[1] = j // MSG
     k = np.arange(256)
     c, i = (k % 128) // 16, k % 16
     var = OWN * c + np.where(k < 128, i % 8, 8 + i % 2)
-    proj = np.arange(VARS)[:, None] == var[None]
     fold = var[:, None] == np.arange(B)[None]
-    return col, proj.astype(BF16), fold.astype(np.float32)
+    return fold.astype(np.float32)
 
 
 def small_grant(mib):
@@ -252,36 +260,46 @@
 
 
 def on_device(cotangent, pair_band, pair_target, pair_count, pair_weight, head_weight, features):
-    col, proj, fold = tables()
+    fold = tables()
     hp_local = features.shape[1]
     place = lax.axis_index(("chan",) + SPACE).astype(jnp.int32).reshape(1)
     hbm = pl.BlockSpec(memory_space=pltpu.HBM)
-    sent = pl.pallas_call(
+    sent, tag_pick, spread, left = pl.pallas_call(
         contribute,
-        out_shape=jax.ShapeDtypeStruct((NSPACE * MSG, B), BF16),
-        in_specs=[pl.BlockSpec(memory_space=pltpu.SMEM)] * 2 + [hbm] * 4,
+        out_shape=(
+            jax.ShapeDtypeStruct((NSPACE * MSG, B), BF16),
+            jax.ShapeDtypeStruct((16, NSPACE * MSG), BF16),
+            jax.ShapeDtypeStruct((SLOTS, NSPACE * MSG), BF16),
+            jax.ShapeDtypeStruct((512, 2 * B), BF16),
+        ),
+        in_specs=[pl.BlockSpec(memory_space=pltpu.SMEM)] * 2 + [hbm] * 5,
         scratch_shapes=[
             pltpu.SMEM((SLOTS,), jnp.int32),
             pltpu.SMEM((SLOTS,), jnp.int32),
             pltpu.VMEM((VARS, BLOCKS * B), BF16),
+            pltpu.VMEM(head_weight.shape, BF16),
             pltpu.VMEM((SLOTS, B, B), BF16),
             pltpu.VMEM((2 * BLOCKS + 1, 16, B), BF16),
             pltpu.VMEM((SLOTS, 16, B), F32),
             pltpu.SMEM((NSPACE,), jnp.int32),
-            pltpu.SemaphoreType.DMA((SLOTS // CHUNK + 3,)),
+            pltpu.SemaphoreType.DMA((SLOTS // CHUNK + 4,)),
         ],
         compiler_params=small_grant(12),
         name="contribute",
-    )(place, pair_count, *map(far, (pair_band, pair_target, cotangent, pair_weight)))
+    )(
+        place,
+        pair_count,
+        *map(far, (pair_band, pair_target, cotangent, head_weight, pair_weight)),
+    )
     got = lax.all_to_all(sent.reshape(NSPACE, MSG // 2, 2, B), SPACE, 0, 0, tiled=True)
     parts = pl.pallas_call(
         collect,
         out_shape=jax.ShapeDtypeStruct((NCHAN, PART, B), BF16),
         in_specs=[pl.BlockSpec(memory_space=pltpu.SMEM)]
-        + [pl.BlockSpec(memory_space=pltpu.VMEM)] * 2,
+        + [pl.BlockSpec(memory_space=pltpu.VMEM)] * 3,
         compiler_params=small_grant(8),
         name="collect",
-    )(place, near(got.reshape(NSPACE * MSG, B)), col)
+    )(place, near(got.reshape(NSPACE * MSG, B)), near(tag_pick), near(spread))
     parts = lax.all_to_all(parts, "chan", 0, 0, tiled=True).reshape(NCHAN * PART, B)
     parts = near(parts)
     feature_grad, share = pl.pallas_call(
@@ -297,7 +315,7 @@
         ],
         compiler_params=small_grant(8),
         name="heads",
-    )(parts, features, head_weight, proj, fold)
+    )(parts, features, near(left), fold)
     share = lax.all_to_all(share, ("x", "core"), 0, 0, tiled=True)
     share = pl.pallas_call(
         add_copies,

time: 75.6 us -> 75.4 us (level)
  no operation moved by 1% of the time
where the time goes in v11:
time: 75.4 us; the launch traced here: 75.1 us
  blocking collectives  68.3 us (91%)
  Pallas kernels  5.38 us (7%)
  between operations  1.38 us (2%)
    all_to_all x1, blocking collectives, on_device(): lax.all_to_all(sent.reshape(NSPACE, MSG // 2, 2, B), SPACE, 0, 0, tiled=T...  24.9 us
    all_to_all x1, blocking collectives, on_device(): lax.all_to_all(parts, 'chan', 0, 0, tiled=True).reshape(NCHAN * PART, B)  22.9 us
    all_to_all x1, blocking collectives, on_device(): share = lax.all_to_all(share, 'y', 0, 0, tiled=True)  10.7 us
    all_to_all x1, blocking collectives, on_device(): share = lax.all_to_all(share, ('x', 'core'), 0, 0, tiled=True)  9.84 us
    pallas_call x1, Pallas kernels, on_device(): pl.pallas_call(contribute, out_shape=(jax.ShapeDtypeStruct((NSPACE * MSG,...  3.08 us

profile of v11, /device:TPU:1, one launch (start us, length us, event | category | flops | bytes accessed | tf_op | source)
XLA Modules:
  0.0 75.1 jit_solution(7640415055715649470)
XLA Ops:
  0.6 0.0 copy-start.1
  0.6 0.0 copy-start
  1.4 3.1 %contribute.1 = (bf16[1408,128]{1,0:T(8,128)(2,1)S(1)}, bf16[16,1408]{1,0:T(8,128)(2,1)S(1)}, bf16[128,1408]{1,0:T(8,128)(2,1)S(1)}, bf16[512,256]{1,0:T(8,128)(2,1)S(1)}) custom-call(s32[1]{0:T(128)} %bitcast.place, s32[1]{0:T(128)S(6)} %copy.10.count, s32[128]{0:T(128)} %band_in.1, s32[128]{0:T(128)} %target_in.1, bf16[80,2048]{1,0:T(8,128)(2,1)} %cot_in.1, ...), custom_call_target="tpu_custom_call" | custom-call | tf_op jit(solution)/shard_map/contribute/pallas_call | solution.py:267
  4.4 24.9 %all_to_all.20 = bf16[64,11,2,128]{3,2,1,0:T(2,128)(2,1)S(1)} all-to-all(bf16[64,11,2,128]{3,2,1,0:T(2,128)(2,1)S(1)} %bitcast.6), channel_id=1, replica_groups=mesh['chan'=8,'y'=8,'x'=4,'core'=2] {'y','x','core'}, dimensions={0} | all-to-all | bytes 720896 | tf_op jit(solution)/shard_map/all_to_all | solution.py:294
  29.3 0.6 collect.1
  29.9 22.9 %all_to_all.21 = bf16[8,160,128]{2,1,0:T(8,128)(2,1)S(1)} all-to-all(bf16[8,160,128]{2,1,0:T(8,128)(2,1)S(1)} %collect.1), channel_id=1, replica_groups=mesh['chan'=8,'y'=8,'x'=4,'core'=2] {'chan'}, dimensions={0} | all-to-all | bytes 655360 | tf_op jit(solution)/shard_map/all_to_all | solution.py:303
  52.9 0.0 copy-done.1
  52.9 0.0 copy-done
  52.9 1.0 %heads.1 = (bf16[64,2048]{1,0:T(8,128)(2,1)}, f32[8,40,128]{2,1,0:T(8,128)S(1)}) custom-call(bf16[1280,128]{1,0:T(8,128)(2,1)S(1)} %bitcast.5, bf16[64,2048]{1,0:T(8,128)(2,1)S(1)} %copy-done, bf16[512,256]{1,0:T(8,128)(2,1)S(1)} %get-tuple-element.11.left, f32[256,128]{1,0:T(8,128)S(1)} %copy-done.1), custom_call_target="tpu_custom_call" | custom-call | tf_op jit(solution)/shard_map/heads/pallas_call | solution.py:305
  53.9 9.8 %all_to_all.22.got = f32[8,40,128]{2,1,0:T(8,128)S(1)} all-to-all(f32[8,40,128]{2,1,0:T(8,128)S(1)} %get-tuple-element.13), channel_id=1, replica_groups=mesh['chan'=8,'y'=8,'x'=4,'core'=2] {'x','core'}, dimensions={0} | all-to-all | bytes 327680 | tf_op jit(solution)/shard_map/all_to_all | solution.py:319
  63.7 10.7 %all_to_all.23.got = f32[8,40,128]{2,1,0:T(8,128)S(1)} all-to-all(f32[8,40,128]{2,1,0:T(8,128)S(1)} %add_copies.1), channel_id=1, replica_groups=mesh['chan'=8,'y'=8,'x'=4,'core'=2] {'y'}, dimensions={0} | all-to-all | bytes 327680 | tf_op jit(solution)/shard_map/all_to_all | solution.py:326
  74.4 0.7 add_last.1
  (1 shorter events, 0.0 us)
Async XLA Ops:
  0.6 52.2 %copy-start.1 = (f32[256,128]{1,0:T(8,128)S(1)}, f32[256,128]{1,0:T(8,128)}, u32[]{:S(2)}) copy-start(f32[256,128]{1,0:T(8,128)} %constant.24.clone.fold) | copy-start | bytes 393220
  0.6 52.2 %copy-start = (bf16[64,2048]{1,0:T(8,128)(2,1)S(1)}, bf16[64,2048]{1,0:T(8,128)(2,1)}, u32[]{:S(2)}) copy-start(bf16[64,2048]{1,0:T(8,128)(2,1)} %features.1) | copy-start | bytes 786436

commit v12 on v11

--- a/solution.py
+++ b/solution.py
@@ -122,7 +122,7 @@
         out[pl.ds(pl.multiple_of(8 * MSG * k, 8 * MSG), 8 * MSG), :] = rows
         return carry
 
-    lax.fori_loop(0, NSPACE // 8, emit, 0)
+    lax.fori_loop(0, NSPACE // 8, emit, 0, unroll=4)
 
 
 def message_columns(place):
@@ -172,12 +172,15 @@
     tails = [gather(16 * k) for k in range(2)]
     mains = [gather(32 + 16 * k) for k in range(8)]
     lane = lax.broadcasted_iota(jnp.int32, (64, B), 1) & 15
-    for pair in range(BLOCKS // 2):
-        two = 128 * (pair % 4)
-        right = jnp.concatenate([mains[pair], tails[pair // 4]], axis=0)
-        both = jnp.dot(left[two : two + 128], right, preferred_element_type=F32).astype(BF16)
-        for k in range(2):
-            grad[:, (2 * pair + k) * B : (2 * pair + k + 1) * B] = both[64 * k : 64 * k + 64]
+    for half in range(2):
+        below = jnp.dot(left[:, B:], tails[half], preferred_element_type=F32)
+        for k in range(4):
+            pair = 4 * half + k
+            both = jnp.dot(left[0 : 2 * 64, 0:B], mains[pair], preferred_element_type=F32)
+            both = (both + below[128 * k : 128 * k + 128]).astype(BF16)
+            for one in range(2):
+                at = (2 * pair + one) * B
+                grad[:, at : at + B] = both[64 * one : 64 * one + 64]
     copy = pltpu.make_async_copy(grad, grad_out, sem)
     copy.start()
 

time: 75.4 us -> 75.4 us (level)
  no operation moved by 1% of the time
where the time goes in v12:
time: 75.4 us; the launch traced here: 75.1 us
  blocking collectives  68.3 us (91%)
  Pallas kernels  5.37 us (7%)
  between operations  1.38 us (2%)
    all_to_all x1, blocking collectives, on_device(): lax.all_to_all(sent.reshape(NSPACE, MSG // 2, 2, B), SPACE, 0, 0, tiled=T...  24.9 us
    all_to_all x1, blocking collectives, on_device(): lax.all_to_all(parts, 'chan', 0, 0, tiled=True).reshape(NCHAN * PART, B)  22.9 us
    all_to_all x1, blocking collectives, on_device(): share = lax.all_to_all(share, 'y', 0, 0, tiled=True)  10.7 us
    all_to_all x1, blocking collectives, on_device(): share = lax.all_to_all(share, ('x', 'core'), 0, 0, tiled=True)  9.84 us
    pallas_call x1, Pallas kernels, on_device(): pl.pallas_call(contribute, out_shape=(jax.ShapeDtypeStruct((NSPACE * MSG,...  3.05 us

profile of v12, /device:TPU:1, one launch (start us, length us, event | category | flops | bytes accessed | tf_op | source)
XLA Modules:
  0.0 75.1 jit_solution(10097570641149712595)
XLA Ops:
  0.6 0.0 copy-start.1
  0.6 0.0 copy-start
  1.4 3.1 %contribute.1 = (bf16[1408,128]{1,0:T(8,128)(2,1)S(1)}, bf16[16,1408]{1,0:T(8,128)(2,1)S(1)}, bf16[128,1408]{1,0:T(8,128)(2,1)S(1)}, bf16[512,256]{1,0:T(8,128)(2,1)S(1)}) custom-call(s32[1]{0:T(128)} %bitcast.place, s32[1]{0:T(128)S(6)} %copy.10.count, s32[128]{0:T(128)} %band_in.1, s32[128]{0:T(128)} %target_in.1, bf16[80,2048]{1,0:T(8,128)(2,1)} %cot_in.1, ...), custom_call_target="tpu_custom_call" | custom-call | tf_op jit(solution)/shard_map/contribute/pallas_call | solution.py:270
  4.4 24.9 %all_to_all.20 = bf16[64,11,2,128]{3,2,1,0:T(2,128)(2,1)S(1)} all-to-all(bf16[64,11,2,128]{3,2,1,0:T(2,128)(2,1)S(1)} %bitcast.6), channel_id=1, replica_groups=mesh['chan'=8,'y'=8,'x'=4,'core'=2] {'y','x','core'}, dimensions={0} | all-to-all | bytes 720896 | tf_op jit(solution)/shard_map/all_to_all | solution.py:297
  29.3 0.6 collect.1
  29.9 22.9 %all_to_all.21 = bf16[8,160,128]{2,1,0:T(8,128)(2,1)S(1)} all-to-all(bf16[8,160,128]{2,1,0:T(8,128)(2,1)S(1)} %collect.1), channel_id=1, replica_groups=mesh['chan'=8,'y'=8,'x'=4,'core'=2] {'chan'}, dimensions={0} | all-to-all | bytes 655360 | tf_op jit(solution)/shard_map/all_to_all | solution.py:306
  52.8 0.0 copy-done.1
  52.8 0.0 copy-done
  52.8 1.0 %heads.1 = (bf16[64,2048]{1,0:T(8,128)(2,1)}, f32[8,40,128]{2,1,0:T(8,128)S(1)}) custom-call(bf16[1280,128]{1,0:T(8,128)(2,1)S(1)} %bitcast.5, bf16[64,2048]{1,0:T(8,128)(2,1)S(1)} %copy-done, bf16[512,256]{1,0:T(8,128)(2,1)S(1)} %get-tuple-element.11.left, f32[256,128]{1,0:T(8,128)S(1)} %copy-done.1), custom_call_target="tpu_custom_call" | custom-call | tf_op jit(solution)/shard_map/heads/pallas_call | solution.py:308
  53.9 9.8 %all_to_all.22.got = f32[8,40,128]{2,1,0:T(8,128)S(1)} all-to-all(f32[8,40,128]{2,1,0:T(8,128)S(1)} %get-tuple-element.13), channel_id=1, replica_groups=mesh['chan'=8,'y'=8,'x'=4,'core'=2] {'x','core'}, dimensions={0} | all-to-all | bytes 327680 | tf_op jit(solution)/shard_map/all_to_all | solution.py:322
  63.7 10.7 %all_to_all.23.got = f32[8,40,128]{2,1,0:T(8,128)S(1)} all-to-all(f32[8,40,128]{2,1,0:T(8,128)S(1)} %add_copies.1), channel_id=1, replica_groups=mesh['chan'=8,'y'=8,'x'=4,'core'=2] {'y'}, dimensions={0} | all-to-all | bytes 327680 | tf_op jit(solution)/shard_map/all_to_all | solution.py:329
  74.4 0.7 add_last.1
  (1 shorter events, 0.0 us)
Async XLA Ops:
  0.6 52.2 %copy-start.1 = (f32[256,128]{1,0:T(8,128)S(1)}, f32[256,128]{1,0:T(8,128)}, u32[]{:S(2)}) copy-start(f32[256,128]{1,0:T(8,128)} %constant.24.clone.fold) | copy-start | bytes 393220
  0.6 52.2 %copy-start = (bf16[64,2048]{1,0:T(8,128)(2,1)S(1)}, bf16[64,2048]{1,0:T(8,128)(2,1)}, u32[]{:S(2)}) copy-start(bf16[64,2048]{1,0:T(8,128)(2,1)} %features.1) | copy-start | bytes 786436

commit v13 on v12

--- a/solution.py
+++ b/solution.py
@@ -152,12 +152,13 @@
 def collect(place, got, tag_pick, spread, out):
     x = got[...]
     at, _, main, rank = message_columns(place)
-    row = lax.broadcasted_iota(jnp.int32, (PART, NSPACE * MSG), 0).astype(F32)
+    row = lax.broadcasted_iota(jnp.int32, (PART, B), 0).astype(F32).astype(BF16)
+    row = jnp.concatenate([row] * (NSPACE * MSG // B), axis=1)
     tags = jnp.dot(tag_pick[...], x, preferred_element_type=F32).astype(BF16)
     label = jnp.dot(tags, spread[...], preferred_element_type=F32)[0:1]
     goal = jnp.where(main, 8 * label + (24 + at - 8 * rank), 2 * label + (at - 18 - 2 * rank))
     goal = jnp.where(label > 0.5, goal, -1.0)
-    route = jnp.where(row == goal, 1.0, 0.0).astype(BF16)
+    route = jnp.where(row == goal.astype(BF16), jnp.ones((), BF16), jnp.zeros((), BF16))
     part = jnp.dot(route, x, preferred_element_type=F32).astype(BF16)
     for j in range(NCHAN):
         out[j] = part

time: 75.4 us -> 75.4 us (level)
  no operation moved by 1% of the time
where the time goes in v13:
time: 75.4 us; the launch traced here: 75.1 us
  blocking collectives  68.3 us (91%)
  Pallas kernels  5.38 us (7%)
  between operations  1.38 us (2%)
    all_to_all x1, blocking collectives, on_device(): lax.all_to_all(sent.reshape(NSPACE, MSG // 2, 2, B), SPACE, 0, 0, tiled=T...  24.9 us
    all_to_all x1, blocking collectives, on_device(): lax.all_to_all(parts, 'chan', 0, 0, tiled=True).reshape(NCHAN * PART, B)  22.9 us
    all_to_all x1, blocking collectives, on_device(): share = lax.all_to_all(share, 'y', 0, 0, tiled=True)  10.7 us
    all_to_all x1, blocking collectives, on_device(): share = lax.all_to_all(share, ('x', 'core'), 0, 0, tiled=True)  9.83 us
    pallas_call x1, Pallas kernels, on_device(): pl.pallas_call(contribute, out_shape=(jax.ShapeDtypeStruct((NSPACE * MSG,...  3.06 us

profile of v13, /device:TPU:1, one launch (start us, length us, event | category | flops | bytes accessed | tf_op | source)
XLA Modules:
  0.0 75.1 jit_solution(18229035062177002220)
XLA Ops:
  0.6 0.0 copy-start.1
  0.6 0.0 copy-start
  1.4 3.1 %contribute.1 = (bf16[1408,128]{1,0:T(8,128)(2,1)S(1)}, bf16[16,1408]{1,0:T(8,128)(2,1)S(1)}, bf16[128,1408]{1,0:T(8,128)(2,1)S(1)}, bf16[512,256]{1,0:T(8,128)(2,1)S(1)}) custom-call(s32[1]{0:T(128)} %bitcast.place, s32[1]{0:T(128)S(6)} %copy.10.count, s32[128]{0:T(128)} %band_in.1, s32[128]{0:T(128)} %target_in.1, bf16[80,2048]{1,0:T(8,128)(2,1)} %cot_in.1, ...), custom_call_target="tpu_custom_call" | custom-call | tf_op jit(solution)/shard_map/contribute/pallas_call | solution.py:271
  4.4 24.9 %all_to_all.20 = bf16[64,11,2,128]{3,2,1,0:T(2,128)(2,1)S(1)} all-to-all(bf16[64,11,2,128]{3,2,1,0:T(2,128)(2,1)S(1)} %bitcast.6), channel_id=1, replica_groups=mesh['chan'=8,'y'=8,'x'=4,'core'=2] {'y','x','core'}, dimensions={0} | all-to-all | bytes 720896 | tf_op jit(solution)/shard_map/all_to_all | solution.py:298
  29.3 0.6 collect.1
  29.9 22.9 %all_to_all.21 = bf16[8,160,128]{2,1,0:T(8,128)(2,1)S(1)} all-to-all(bf16[8,160,128]{2,1,0:T(8,128)(2,1)S(1)} %collect.1), channel_id=1, replica_groups=mesh['chan'=8,'y'=8,'x'=4,'core'=2] {'chan'}, dimensions={0} | all-to-all | bytes 655360 | tf_op jit(solution)/shard_map/all_to_all | solution.py:307
  52.8 0.0 copy-done.1
  52.8 0.0 copy-done
  52.8 1.0 %heads.1 = (bf16[64,2048]{1,0:T(8,128)(2,1)}, f32[8,40,128]{2,1,0:T(8,128)S(1)}) custom-call(bf16[1280,128]{1,0:T(8,128)(2,1)S(1)} %bitcast.5, bf16[64,2048]{1,0:T(8,128)(2,1)S(1)} %copy-done, bf16[512,256]{1,0:T(8,128)(2,1)S(1)} %get-tuple-element.11.left, f32[256,128]{1,0:T(8,128)S(1)} %copy-done.1), custom_call_target="tpu_custom_call" | custom-call | tf_op jit(solution)/shard_map/heads/pallas_call | solution.py:309
  53.9 9.8 %all_to_all.22.got = f32[8,40,128]{2,1,0:T(8,128)S(1)} all-to-all(f32[8,40,128]{2,1,0:T(8,128)S(1)} %get-tuple-element.13), channel_id=1, replica_groups=mesh['chan'=8,'y'=8,'x'=4,'core'=2] {'x','core'}, dimensions={0} | all-to-all | bytes 327680 | tf_op jit(solution)/shard_map/all_to_all | solution.py:323
  63.7 10.7 %all_to_all.23.got = f32[8,40,128]{2,1,0:T(8,128)S(1)} all-to-all(f32[8,40,128]{2,1,0:T(8,128)S(1)} %add_copies.1), channel_id=1, replica_groups=mesh['chan'=8,'y'=8,'x'=4,'core'=2] {'y'}, dimensions={0} | all-to-all | bytes 327680 | tf_op jit(solution)/shard_map/all_to_all | solution.py:330
  74.4 0.7 add_last.1
  (1 shorter events, 0.0 us)
Async XLA Ops:
  0.6 52.2 %copy-start.1 = (f32[256,128]{1,0:T(8,128)S(1)}, f32[256,128]{1,0:T(8,128)}, u32[]{:S(2)}) copy-start(f32[256,128]{1,0:T(8,128)} %constant.24.clone.fold) | copy-start | bytes 393220
  0.6 52.2 %copy-start = (bf16[64,2048]{1,0:T(8,128)(2,1)S(1)}, bf16[64,2048]{1,0:T(8,128)(2,1)}, u32[]{:S(2)}) copy-start(bf16[64,2048]{1,0:T(8,128)(2,1)} %features.1) | copy-start | bytes 786436
